TPU v7x, 512 devices: a whole 4x4x16 slice. The times are simulated.
512 devices in a mesh: seq: 64 (over y, x, z_hi), head: 8 (over z_lo, core).
Axes of the slice: x: 4, y: 4, z: 16 (z_hi: 4, z_lo: 4; z = z_hi * 4 + z_lo), core: 2. Of those that a mesh axis runs over, the one named last changes fastest.
Arguments:
- inputs: bfloat16 [32768, 4096], P('seq', 'head'), may hold values from -6 to 6
- latent: float32 [4096, 2048], P('seq', 'head'), as said below
- queries: bfloat16 [32768, 2048], P('seq', 'head'), may hold values from -6 to 6
- keys: bfloat16 [32768, 2048], P('seq', 'head'), may hold values from -6 to 6
- grad_out: bfloat16 [32768, 2048], P('seq', 'head'), may hold values from -6 to 6
Outputs:
- attn_out: bfloat16 [32768, 2048], P('seq', 'head')
- grad_queries: bfloat16 [32768, 2048], P('seq', 'head')
- grad_keys: bfloat16 [32768, 2048], P('seq', 'head')
- grad_latent: float32 [4096, 2048], P('seq', 'head')
Inputs may be any that keep to these rules, and one draw needn't show every extreme that they name: `latent`: no entry's magnitude lies between 0.67 and 1.5 times half of its column's mean magnitude.
All inputs are finite; a program needn't handle non-finite values.
Results may differ from a plain program's by a relative error of at most 0.014.
Values may be sent and summed in bfloat16 or wider, within the bound.
A program may use at most 64 MiB of HBM per device.

v0:
```python
import jax
import jax.numpy as jnp
from jax import lax
from jax.sharding import Mesh
from jax.sharding import PartitionSpec as P

DK = 128
BLOCK = 128
HEAD = ("head_0", "head_1")
SEQ = ("seq_0", "seq_1", "seq_2")


absmean_eps = 1e-05
norm_eps = 1e-06


def from_everyone(array, axis):
    count = lax.axis_size(axis)
    return lax.all_to_all(
        jnp.broadcast_to(array[None], (count, *array.shape)), axis, 0, 0, tiled=True
    )


def joined_along(pieces, dim):
    lengths = list(pieces.shape[1:])
    lengths[dim] *= pieces.shape[0]
    return jnp.moveaxis(pieces, 0, dim).reshape(lengths)


def gather_axes(array, axes, dim):
    far, near = axes
    initial = from_everyone(array, far)
    pieces = jnp.swapaxes(from_everyone(initial, near), 0, 1)
    return joined_along(pieces.reshape(-1, *array.shape), dim)


def filled_with(array, identity):
    return jnp.broadcast_to(jnp.asarray(identity, array.dtype), array.shape)


def prefix_by_axis(array, axes, combine, identity, reverse):
    before = start = filled_with(array, identity)
    so_far = array
    for axis in reversed(axes):
        count, position = (lax.axis_size(axis), lax.axis_index(axis))
        pieces = lax.all_gather(so_far.astype(jnp.bfloat16), axis)
        inside, so_far = (start, start)
        for k in reversed(range(count)) if reverse else range(count):
            passed = k > position if reverse else k < position
            so_far = combine(so_far, pieces[k].astype(array.dtype))
            inside = jnp.where(passed, so_far, inside)
        before = combine(inside, before)
    return before


def split_up(array, dim, count):
    lengths = array.shape
    pieces = array.reshape(*lengths[:dim], count, lengths[dim] // count, *lengths[dim + 1 :])
    return jnp.moveaxis(pieces, dim, 0)


def sum_at_owner(array, axis, dim):
    pieces = split_up(array, dim, lax.axis_size(axis))
    arrived = lax.all_to_all(pieces, axis, split_axis=0, concat_axis=0, tiled=True)
    return arrived.sum(axis=0)


def summed_rows(array, axes, dim):
    far, near = axes
    return sum_at_owner(sum_at_owner(array, far, dim), near, dim)


def ternarize(weights, column_scale):
    halfway = 0.5 * column_scale
    ternary_signs = jnp.where(weights > halfway, 1.0, jnp.where(weights < -halfway, -1.0, 0.0))
    return (ternary_signs * column_scale).astype(jnp.bfloat16)


def blocked(matrix, head_count):
    return matrix.reshape(matrix.shape[0] // BLOCK, BLOCK, head_count, DK)


def add_states(earlier, follows):
    return earlier + follows


def split_pair(state):
    upper = state.astype(jnp.bfloat16)
    lower = (state - upper.astype(jnp.float32)).astype(jnp.bfloat16)
    return (upper, lower)


def state_product(form, operand, state_pair):
    first = jnp.einsum(form, operand, state_pair[0], preferred_element_type=jnp.float32)
    return first + jnp.einsum(form, operand, state_pair[1], preferred_element_type=jnp.float32)


def per_device(inputs, latent, queries, keys, grad_out):
    columns = latent.shape[1]
    head_count = columns // DK
    tokens = inputs.shape[0]
    features_all = gather_axes(inputs, ("head_0", "head_1"), 1)
    full_latent = lax.all_gather(latent.astype(jnp.bfloat16), SEQ, axis=0, tiled=True).astype(
        latent.dtype
    )
    column_scale = jnp.mean(jnp.abs(full_latent), axis=0) + absmean_eps
    projected = jnp.dot(
        features_all, ternarize(full_latent, column_scale), preferred_element_type=jnp.float32
    )
    query_blocks = blocked(queries, head_count)
    key_blocks = blocked(keys, head_count)
    value_blocks = blocked(projected.astype(jnp.bfloat16), head_count)
    causal = jnp.tril(jnp.ones((BLOCK, BLOCK), jnp.bool_))
    scores = jnp.where(
        causal,
        jnp.einsum("bthd,bshd->bhts", query_blocks, key_blocks, preferred_element_type=jnp.float32),
        0.0,
    ).astype(jnp.bfloat16)
    within = jnp.einsum("bhts,bshd->bthd", scores, value_blocks, preferred_element_type=jnp.float32)
    block_states = jnp.einsum(
        "bshd,bshe->bhde", key_blocks, value_blocks, preferred_element_type=jnp.float32
    )
    local_total = jnp.sum(block_states, axis=0)
    incoming = prefix_by_axis(local_total, SEQ, add_states, jnp.zeros_like(local_total), False)
    prior = incoming[None] + (jnp.cumsum(block_states, axis=0) - block_states)
    prior_pair = split_pair(prior)
    across = state_product("bthd,bhde->bthe", query_blocks, prior_pair)
    mixed = within + across
    root_mean = jnp.sqrt(jnp.mean(mixed * mixed, axis=-1, keepdims=True) + norm_eps)
    normed = mixed / root_mean
    attn_out = normed.astype(jnp.bfloat16).reshape(tokens, columns)
    upstream = blocked(grad_out, head_count).astype(jnp.float32)
    inner_mean = jnp.mean(upstream * normed, axis=-1, keepdims=True)
    grad_mixed = ((upstream - normed * inner_mean) / root_mean).astype(jnp.bfloat16)
    grad_states = jnp.einsum(
        "bthd,bthe->bhde", query_blocks, grad_mixed, preferred_element_type=jnp.float32
    )
    grad_total = jnp.sum(grad_states, axis=0)
    arriving = prefix_by_axis(grad_total, SEQ, add_states, jnp.zeros_like(grad_total), True)
    following = arriving[None] + (grad_total[None] - jnp.cumsum(grad_states, axis=0))
    following_pair = split_pair(following)
    grad_scores = jnp.where(
        causal,
        jnp.einsum("bthe,bshe->bhts", grad_mixed, value_blocks, preferred_element_type=jnp.float32),
        0.0,
    ).astype(jnp.bfloat16)
    grad_query = jnp.einsum(
        "bhts,bshd->bthd", grad_scores, key_blocks, preferred_element_type=jnp.float32
    ) + state_product("bthe,bhde->bthd", grad_mixed, prior_pair)
    grad_key = jnp.einsum(
        "bhts,bthd->bshd", grad_scores, query_blocks, preferred_element_type=jnp.float32
    ) + state_product("bshe,bhde->bshd", value_blocks, following_pair)
    grad_value = jnp.einsum(
        "bhts,bthe->bshe", scores, grad_mixed, preferred_element_type=jnp.float32
    ) + state_product("bshd,bhde->bshe", key_blocks, following_pair)
    grad_flat = grad_value.astype(jnp.bfloat16).reshape(tokens, columns)
    weight_term = lax.dot_general(
        features_all, grad_flat, (((0,), (0,)), ((), ())), preferred_element_type=jnp.float32
    )
    grad_latent = summed_rows(weight_term, (("seq_0", "seq_1"), "seq_2"), 0)
    grad_queries = grad_query.astype(jnp.bfloat16).reshape(tokens, columns)
    grad_keys = grad_key.astype(jnp.bfloat16).reshape(tokens, columns)
    return (attn_out, grad_queries, grad_keys, grad_latent)


def solution(mesh):
    torus = Mesh(
        mesh.devices.reshape(4, 4, 4, 4, 2), ("seq_0", "seq_1", "seq_2", "head_0", "head_1")
    )
    placed = (P(SEQ, HEAD), P(SEQ, HEAD), P(SEQ, HEAD), P(SEQ, HEAD), P(SEQ, HEAD))
    return jax.shard_map(
        per_device,
        mesh=torus,
        in_specs=placed,
        out_specs=(P(SEQ, HEAD), P(SEQ, HEAD), P(SEQ, HEAD), P(SEQ, HEAD)),
        check_vma=False,
    )
```

profile of v0, /device:TPU:6, one launch (start us, length us, event | category | flops | bytes accessed | tf_op | source)
XLA Modules:
  0.0 355.7 jit_solution(429812832664177441)
XLA Ops:
  7.2 2.6 broadcast_in_dim.50
  9.8 5.9 %all-to-all-start = ((bf16[4,512,512]{2,1,0:T(8,128)(2,1)}), bf16[4,512,512]{2,1,0:T(8,128)(2,1)S(1)}, u32[]{:S(2)}, u32[]{:S(2)}) async-start(bf16[4,512,512]{2,1,0:T(8,128)(2,1)} %broadcast_in_dim.50), calls=%async_computation | async-start | bytes 4194304 | tf_op jit(solution)/shard_map/all_to_all | solution.py:19
  17.0 1.0 reshape.88
  18.4 132.7 %all-gather.4.cloned.1.call-done = bf16[4096,256]{1,0:T(8,128)(2,1)} async-done(((bf16[64,256]{1,0:T(8,128)(2,1)}), bf16[4096,256]{1,0:T(8,128)(2,1)}) %all-gather.4.cloned.1.call-update) | async-done | bytes 2097168 | tf_op jit(solution)/shard_map/all_gather | solution.py:103
  151.1 2.2 fusion
  153.7 7.1 %all_to_all.20 = bf16[2,4,512,512]{3,2,1,0:T(8,128)(2,1)S(1)} all-to-all(bf16[2,4,512,512]{3,2,1,0:T(8,128)(2,1)S(1)} %broadcast_in_dim.51), channel_id=1, replica_groups=mesh['seq_0'=4,'seq_1'=4,'seq_2'=4,'head_0'=4,'head_1'=2] {'head_1'}, dimensions={0} | all-to-all | bytes 8388608 | tf_op jit(solution)/shard_map/all_to_all | solution.py:19
  160.8 2.4 copy.151
  163.2 6.6 %copy.152 = bf16[512,8,512]{0,2,1:T(8,128)(2,1)} copy(bf16[512,8,512]{2,0,1:T(8,128)(2,1)} %bitcast.96) | data formatting | bytes 8388608 | tf_op jit(solution)/shard_map/transpose | solution.py:27
  169.8 4.2 %fusion.23 = bf16[512,256]{0,1:T(8,128)(2,1)} fusion(bf16[512,4096]{0,1:T(8,128)(2,1)} %bitcast.92, bf16[4096,256]{1,0:T(8,128)(2,1)S(1)} %copy-done.1, f32[256]{0:T(256)S(1)} %get-tuple-element.8, f32[256]{0:T(256)S(1)} %get-tuple-element.7, f32[256]{0:T(256)S(1)} %get-tuple-element.6), kind=kOutput, calls=%fused_computation.40 | convolution fusion | flops 1081212928 | bytes 6556672 | tf_op jit(solution)/shard_map/dot_general | solution.py:107
  174.0 1.0 reshape.87
  175.5 1.1 fusion.85
  176.8 18.8 %all-gather = bf16[8,128,128]{2,1,0:T(8,128)(2,1)S(1)} all-gather(bf16[2,128,128]{2,1,0:T(8,128)(2,1)S(1)} %copy.158), channel_id=2, replica_groups=mesh['seq_0'=4,'seq_1'=4,'seq_2'=4,'head_0'=4,'head_1'=2] {'seq_2'}, dimensions={0}, use_global_device_ids=true | all-gather | bytes 327680 | tf_op jit(solution)/shard_map/all_gather | solution.py:46
  195.7 12.3 %all_gather.29 = bf16[4,2,128,128]{3,2,1,0:T(8,128)(2,1)S(1)} all-gather(bf16[1,2,128,128]{3,2,1,0:T(8,128)(2,1)S(1)} %fusion.70), channel_id=1, replica_groups=mesh['seq_0'=4,'seq_1'=4,'seq_2'=4,'head_0'=4,'head_1'=2] {'seq_1'}, dimensions={0}, use_global_device_ids=true | all-gather | bytes 327680 | tf_op jit(solution)/shard_map/all_gather | solution.py:46
  208.0 13.2 %all_gather.30 = bf16[4,2,128,128]{3,2,1,0:T(8,128)(2,1)S(1)} all-gather(bf16[1,2,128,128]{3,2,1,0:T(8,128)(2,1)S(1)} %fusion.69), channel_id=1, replica_groups=mesh['seq_0'=4,'seq_1'=4,'seq_2'=4,'head_0'=4,'head_1'=2] {'seq_0'}, dimensions={0}, use_global_device_ids=true | all-gather | bytes 327680 | tf_op jit(solution)/shard_map/all_gather | solution.py:46
  221.9 1.4 multiply_reduce_fusion.1
  223.4 0.8 divide_convert_fusion
  224.8 18.6 %all-gather.1 = bf16[8,128,128]{2,1,0:T(8,128)(2,1)S(1)} all-gather(bf16[2,128,128]{2,1,0:T(8,128)(2,1)S(1)} %copy.178), channel_id=3, replica_groups=mesh['seq_0'=4,'seq_1'=4,'seq_2'=4,'head_0'=4,'head_1'=2] {'seq_2'}, dimensions={0}, use_global_device_ids=true | all-gather | bytes 327680 | tf_op jit(solution)/shard_map/all_gather | solution.py:46
  243.4 12.3 %all_gather.32 = bf16[4,2,128,128]{3,2,1,0:T(8,128)(2,1)S(1)} all-gather(bf16[1,2,128,128]{3,2,1,0:T(8,128)(2,1)S(1)} %fusion.71), channel_id=1, replica_groups=mesh['seq_0'=4,'seq_1'=4,'seq_2'=4,'head_0'=4,'head_1'=2] {'seq_1'}, dimensions={0}, use_global_device_ids=true | all-gather | bytes 327680 | tf_op jit(solution)/shard_map/all_gather | solution.py:46
  255.7 12.3 %all_gather.33 = bf16[4,2,128,128]{3,2,1,0:T(8,128)(2,1)S(1)} all-gather(bf16[1,2,128,128]{3,2,1,0:T(8,128)(2,1)S(1)} %fusion.68), channel_id=1, replica_groups=mesh['seq_0'=4,'seq_1'=4,'seq_2'=4,'head_0'=4,'head_1'=2] {'seq_0'}, dimensions={0}, use_global_device_ids=true | all-gather | bytes 327680 | tf_op jit(solution)/shard_map/all_gather | solution.py:46
  269.2 3.5 fusion.25
  272.7 2.4 copy.245
  275.1 6.5 %all-to-all-start.2 = ((f32[16,256,256]{1,2,0:T(8,128)}), f32[16,256,256]{1,2,0:T(8,128)}, u32[]{:S(2)}, u32[]{:S(2)}) async-start(f32[16,256,256]{1,2,0:T(8,128)} %bitcast.94), calls=%async_computation.2 | async-start | bytes 8388608 | tf_op jit(solution)/shard_map/all_to_all | solution.py:64
  282.5 1.1 fusion.11
  283.5 40.9 %all-to-all-done.2 = f32[16,256,256]{1,2,0:T(8,128)} async-done(((f32[16,256,256]{1,2,0:T(8,128)}), f32[16,256,256]{1,2,0:T(8,128)}, u32[]{:S(2)}, u32[]{:S(2)}) %all-to-all-start.2) | async-done | bytes 4194336 | tf_op jit(solution)/shard_map/all_to_all | solution.py:64
  324.4 2.5 reduce_sum.68
  326.9 0.8 copy.192
  327.7 6.6 %all-to-all-start.3 = ((f32[4,64,256]{2,1,0:T(8,128)}), f32[4,64,256]{2,1,0:T(8,128)S(1)}, u32[]{:S(2)}, u32[]{:S(2)}) async-start(f32[4,64,256]{2,1,0:T(8,128)} %bitcast.20), calls=%async_computation.3 | async-start | bytes 524288 | tf_op jit(solution)/shard_map/all_to_all | solution.py:64
  334.7 1.1 copy.162
  335.8 0.7 copy.246
  337.6 0.9 copy_bitcast_fusion.1
  338.4 9.8 %all-to-all-done.3 = f32[4,64,256]{2,1,0:T(8,128)S(1)} async-done(((f32[4,64,256]{2,1,0:T(8,128)}), f32[4,64,256]{2,1,0:T(8,128)S(1)}, u32[]{:S(2)}, u32[]{:S(2)}) %all-to-all-start.3) | async-done | bytes 262176 | tf_op jit(solution)/shard_map/all_to_all | solution.py:64
  348.3 0.6 reduce_sum.69
  (53 shorter events, 7.4 us)
Async XLA Ops:
  7.2 8.5 %copy-start.4 = (f32[64,256]{1,0:T(8,128)S(1)}, f32[64,256]{1,0:T(8,128)}, u32[]{:S(2)}) copy-start(f32[64,256]{1,0:T(8,128)} %param.6) | copy-start | bytes 196612
  7.2 9.3 %copy-start.2 = (bf16[512,256]{1,0:T(8,128)(2,1)S(1)}, bf16[512,256]{1,0:T(8,128)(2,1)}, u32[]{:S(2)}) copy-start(bf16[512,256]{1,0:T(8,128)(2,1)} %param.9) | copy-start | bytes 786436
  7.2 9.8 %copy-start.3 = (bf16[512,256]{1,0:T(8,128)(2,1)S(1)}, bf16[512,256]{1,0:T(8,128)(2,1)}, u32[]{:S(2)}) copy-start(bf16[512,256]{1,0:T(8,128)(2,1)} %param.8) | copy-start | bytes 786436
  9.8 143.4 %all-to-all-start = ((bf16[4,512,512]{2,1,0:T(8,128)(2,1)}), bf16[4,512,512]{2,1,0:T(8,128)(2,1)S(1)}, u32[]{:S(2)}, u32[]{:S(2)}) async-start(bf16[4,512,512]{2,1,0:T(8,128)(2,1)} %broadcast_in_dim.50), calls=%async_computation | async-start | bytes 4194304 | tf_op jit(solution)/shard_map/all_to_all | solution.py:19
  15.7 135.4 %all-gather.4.cloned.1.call-start = ((), (), s32[]{:S(2)}) async-start(), calls=%async_computation.4 | async-start | bytes 2129920 | tf_op jit(solution)/shard_map/all_gather | solution.py:103
  163.2 6.6 %copy-start.1 = (bf16[4096,256]{1,0:T(8,128)(2,1)S(1)}, bf16[4096,256]{1,0:T(8,128)(2,1)}, u32[]{:S(2)}) copy-start(bf16[4096,256]{1,0:T(8,128)(2,1)} %all-gather.4.cloned.1.call-done) | copy-start | bytes 6291460
  275.1 49.3 %all-to-all-start.2 = ((f32[16,256,256]{1,2,0:T(8,128)}), f32[16,256,256]{1,2,0:T(8,128)}, u32[]{:S(2)}, u32[]{:S(2)}) async-start(f32[16,256,256]{1,2,0:T(8,128)} %bitcast.94), calls=%async_computation.2 | async-start | bytes 8388608 | tf_op jit(solution)/shard_map/all_to_all | solution.py:64
  283.5 50.8 %copy-start = (f32[4,128,2,128]{3,1,2,0:T(8,128)S(1)}, f32[4,128,2,128]{3,1,2,0:T(8,128)}, u32[]{:S(2)}) copy-start(f32[4,128,2,128]{3,1,2,0:T(8,128)} %fusion.11) | copy-start | bytes 1572868
  327.7 20.5 %all-to-all-start.3 = ((f32[4,64,256]{2,1,0:T(8,128)}), f32[4,64,256]{2,1,0:T(8,128)S(1)}, u32[]{:S(2)}, u32[]{:S(2)}) async-start(f32[4,64,256]{2,1,0:T(8,128)} %bitcast.20), calls=%async_computation.3 | async-start | bytes 524288 | tf_op jit(solution)/shard_map/all_to_all | solution.py:64
Sparse Core Ops, SparseCore 0:
  21.3 129.7 all-gather.3
where the time goes:
time: 358 us; the launch traced here: 356 us
  waiting for transfers between devices  183 us (51%)
  blocking collectives  94.5 us (26%)
  local copies, waits for them, and re-layouts  22 us (6%)
  starting transfers between devices  19.1 us (5%)
  matrix products  14.8 us (4%)
  between operations  14.4 us (4%)
  other arithmetic  7.57 us (2%)
    all_gather x1, waiting for transfers between devices, per_device(): lax.all_gather(latent.astype(jnp.bfloat16), SEQ, axis=0, tiled=True)  133 us
    all_gather x6, blocking collectives, prefix_by_axis(): pieces = lax.all_gather(so_far.astype(jnp.bfloat16), axis)  87.4 us
    all_to_all x2, waiting for transfers between devices, sum_at_owner(): lax.all_to_all(pieces, axis, split_axis=0, concat_axis=0, tiled=True)  50.7 us
    all_to_all x2, starting transfers between devices, sum_at_owner(): lax.all_to_all(pieces, axis, split_axis=0, concat_axis=0, tiled=True)  13.2 us
  transfers between devices with their start and end apart: 4, of which 3 were waited for; matrix products, arithmetic and copies ran while one was open for 3% of the time, Pallas kernels for 0%

commit v1 on v0

v1 whole, which is shorter than its diff:
```python
import functools

import jax
import jax.numpy as jnp
from jax import lax
from jax.experimental import pallas as pl
from jax.experimental.pallas import tpu as pltpu
from jax.sharding import Mesh
from jax.sharding import PartitionSpec as P

DK = 128
BLOCK = 128
HEAD = ("head_0", "head_1")
SEQ = ("seq_0", "seq_1", "seq_2")
ID = pl.DeviceIdType.MESH
CHUNKS = 4

absmean_eps = 1e-05
norm_eps = 1e-06

f32 = jnp.float32
bf16 = jnp.bfloat16


def dot(a, b, contract):
    return lax.dot_general(a, b, ((contract[:1], contract[1:]), ((), ())), preferred_element_type=f32)


NN, NT, TN = (1, 0), (1, 1), (0, 0)


def exchange(axis, count, source, target, send, recv):
    position = lax.axis_index(axis)
    copies = []
    for kk in range(1, count):
        peer = lax.rem(position + kk, count)
        copy = pltpu.make_async_remote_copy(
            src_ref=source(peer),
            dst_ref=target(kk),
            send_sem=send.at[kk - 1],
            recv_sem=recv.at[kk - 1],
            device_id={axis: peer},
            device_id_type=ID,
        )
        copy.start()
        copies.append(copy)
    return copies


def arrive(copies):
    for copy in copies:
        copy.wait_recv()


def kernel(
    sizes, x_ref, latent_ref, q_ref, k_ref, go_ref, attn_ref, gq_ref, gk_ref, gl_ref,
    wa, wb, wt, xg, acc, v, sc, st, prior, within, gm, gs, gkp, gvp, gvt, loc, scan_send, scan_recv, inc,
    pa, pb, ra1, rb1, sa2, sb2, ra2, rb2, tz, tzf, rz,
    own_sem, wz_s, wz_r, w2_s, w2_r, w3_s, w3_r, xp_s, xm_s, xs_s, xl_r, xs_r, scan_s, scan_r, g_s, g_r,
):
    ny, nx, nz, nl = sizes
    yy, xx, zh = (lax.axis_index(a) for a in SEQ)
    zl, cc = (lax.axis_index(a) for a in HEAD)
    tokens, feats = x_ref.shape
    rows, columns = latent_ref.shape
    half = rows // 2
    heads = columns // DK
    blocks = tokens // BLOCK
    step = tokens // CHUNKS
    sent = []

    own_x = pltpu.make_async_copy(x_ref, xg.at[zl, cc], own_sem)
    own_x.start()
    at_a = (yy * nx + xx) * nz
    at_b = (xx * ny + yy) * nz
    latent16 = latent_ref[...].astype(bf16)
    wa[at_a + zh] = latent16[:half]
    wb[at_b + zh] = latent16[half:]

    barrier = pltpu.get_barrier_semaphore()
    for axis, count in (("seq_2", nz), ("seq_1", nx), ("seq_0", ny), ("head_1", 2)):
        position = lax.axis_index(axis)
        for kk in range(1, count):
            pl.semaphore_signal(
                barrier, inc=1, device_id={axis: lax.rem(position + kk, count)}, device_id_type=ID
            )

    @pl.when(zl > 0)
    def _():
        pl.semaphore_signal(barrier, inc=1, device_id={"head_0": zl - 1}, device_id_type=ID)

    @pl.when(zl < nl - 1)
    def _():
        pl.semaphore_signal(barrier, inc=1, device_id={"head_0": zl + 1}, device_id_type=ID)

    partners = (nz - 1) + (nx - 1) + (ny - 1) + 1
    neighbours = jnp.where(zl > 0, 1, 0) + jnp.where(zl < nl - 1, 1, 0)
    pl.semaphore_wait(barrier, partners + neighbours)

    wz = exchange("seq_2", nz, lambda p: wa.at[at_a + zh], lambda kk: wa.at[at_a + zh], wz_s.at[0], wz_r.at[0])
    wz += exchange("seq_2", nz, lambda p: wb.at[at_b + zh], lambda kk: wb.at[at_b + zh], wz_s.at[1], wz_r.at[1])
    sent += wz

    def rows_of(ref, j):
        return ref.at[pl.ds(pl.multiple_of(j * step, step), step)]

    def line_copy(block, j, up, own):
        place = rows_of(xg.at[block, cc], j)
        return pltpu.make_async_remote_copy(
            src_ref=rows_of(x_ref, j) if own else place,
            dst_ref=place,
            send_sem=(xp_s if up else xm_s).at[block, j],
            recv_sem=xl_r.at[block, j],
            device_id={"head_0": zl + 1 if up else zl - 1},
            device_id_type=ID,
        )

    def side_copy(block, j, own):
        place = rows_of(xg.at[block, cc], j)
        return pltpu.make_async_remote_copy(
            src_ref=rows_of(x_ref, j) if own else place,
            dst_ref=place,
            send_sem=xs_s.at[block, j],
            recv_sem=xs_r.at[block, j],
            device_id={"head_1": 1 - cc},
            device_id_type=ID,
        )

    @pl.loop(0, CHUNKS)
    def _(j):
        @pl.when(zl < nl - 1)
        def _():
            line_copy(zl, j, True, True).start()

        @pl.when(zl > 0)
        def _():
            line_copy(zl, j, False, True).start()

    @pl.loop(0, CHUNKS)
    def _(j):
        side_copy(zl, j, True).start()

    def relay(distance):
        @pl.loop(0, CHUNKS)
        def _(j):
            @pl.when(zl >= distance)
            def _():
                block = zl - distance
                line_copy(block, j, True, False).wait_recv()

                @pl.when(zl < nl - 1)
                def _():
                    line_copy(block, j, True, False).start()

                side_copy(block, j, False).start()

            @pl.when(zl + distance < nl)
            def _():
                block = zl + distance
                line_copy(block, j, False, False).wait_recv()

                @pl.when(zl > 0)
                def _():
                    line_copy(block, j, False, False).start()

                side_copy(block, j, False).start()

    causal = lax.broadcasted_iota(jnp.int32, (BLOCK, BLOCK), 0) >= lax.broadcasted_iota(
        jnp.int32, (BLOCK, BLOCK), 1
    )

    def each_block(body):
        @pl.loop(0, blocks)
        def _(b):
            at = pl.ds(pl.multiple_of(b * BLOCK, BLOCK), BLOCK)
            for i in range(heads):
                body(b, i, at, slice(i * DK, (i + 1) * DK))

    def scores_body(b, i, at, cols):
        s = dot(q_ref[at, cols], k_ref[at, cols], NT)
        sc[b, i] = jnp.where(causal, s, 0.0).astype(bf16)

    each_block(scores_body)

    arrive(wz)
    mine_a = wa.at[pl.ds(at_a, nz)]
    mine_b = wb.at[pl.ds(at_b, nz)]
    w2a = exchange("seq_1", nx, lambda p: mine_a, lambda kk: mine_a, w2_s.at[0], w2_r.at[0])
    w2b = exchange("seq_0", ny, lambda p: mine_b, lambda kk: mine_b, w2_s.at[1], w2_r.at[1])
    sent += w2a + w2b
    relay(1)
    row_a = wa.at[pl.ds(yy * nx * nz, nx * nz)]
    row_b = wb.at[pl.ds(xx * ny * nz, ny * nz)]
    arrive(w2a)
    w3a = exchange("seq_0", ny, lambda p: row_a, lambda kk: row_a, w3_s.at[0], w3_r.at[0])
    arrive(w2b)
    w3b = exchange("seq_1", nx, lambda p: row_b, lambda kk: row_b, w3_s.at[1], w3_r.at[1])
    sent += w3a + w3b
    for distance in range(2, nl - 1):
        relay(distance)
    arrive(w3a)
    arrive(w3b)

    def magnitude(s, total):
        both = jnp.abs(wa[s].astype(f32)) + jnp.abs(wb[s].astype(f32))
        return total + both.reshape(half // 8, 8, columns).sum(axis=0)

    total = lax.fori_loop(0, ny * nx * nz, magnitude, jnp.zeros((8, columns), f32))
    scale = total.sum(axis=0, keepdims=True) / (ny * nx * nz * rows) + absmean_eps
    halfway = 0.5 * scale

    def ternary(w):
        w = w.astype(f32)
        return jnp.where(w > halfway, scale, jnp.where(w < -halfway, -scale, 0.0)).astype(bf16)

    @pl.loop(0, ny * nx)
    def _(p):
        other = lax.rem(p, nx) * ny + p // nx
        for z in range(nz):
            at = pl.multiple_of((p * nz + z) * rows, rows)
            wt[pl.ds(at, half)] = ternary(wa[p * nz + z])
            wt[pl.ds(pl.multiple_of(at + half, half), half)] = ternary(wb[other * nz + z])

    relay(nl - 1)
    own_x.wait()

    @pl.loop(0, nl)
    def _(block):
        @pl.loop(0, CHUNKS)
        def _(j):
            side_copy(block, j, False).wait_recv()

    acc[...] = jnp.zeros_like(acc)

    @pl.loop(0, nl * 2)
    def _(h):
        at = pl.ds(pl.multiple_of(h * feats, feats), feats)
        acc[...] += dot(xg[h // 2, lax.rem(h, 2)], wt[at], NN)

    v[...] = acc[...].astype(bf16)

    for i in range(heads):
        loc[i] = jnp.zeros((DK, DK), f32)

    def state_body(b, i, at, cols):
        s = dot(k_ref[at, cols], v[at, cols], TN)
        st[b, i] = s
        loc[i] += s

    each_block(state_body)

    def scan(which, reverse):
        def earlier(p, mine):
            return p > mine if reverse else p < mine

        send, recv = scan_send.at[which], scan_recv.at[which]

        def go(axis, count, i, stage, source):
            slot = i * 3 + stage
            copies = exchange(
                axis, count, source, lambda kk: recv.at[slot, kk - 1],
                scan_s.at[which, slot], scan_r.at[which, slot],
            )
            sent.extend(copies)
            return copies

        def collect(axis, count, i, stage, copies, mine):
            position = lax.axis_index(axis)
            before, everything = jnp.zeros((DK, DK), f32), mine
            for kk in range(1, count):
                copies[kk - 1].wait_recv()
                value = recv[i * 3 + stage, kk - 1].astype(f32)
                sender = lax.rem(position + count - kk, count)
                before += jnp.where(earlier(sender, position), value, 0.0)
                everything += value
            return before, everything

        def plain(slot, value):
            send[slot, 0] = value.astype(bf16)
            return lambda p: send.at[slot, 0]

        ax = go("seq_1", nx, 0, 0, plain(0, loc[0]))
        bz = go("seq_2", nz, 1, 0, plain(3, loc[1]))
        before_a, row = collect("seq_1", nx, 0, 0, ax, loc[0])
        ay = go("seq_0", ny, 0, 1, plain(1, row))
        more, _ = collect("seq_0", ny, 0, 1, ay, row)
        before_a += more
        send[2, 0] = before_a.astype(bf16)
        send[2, 1] = (before_a + loc[0]).astype(bf16)
        az = go("seq_2", nz, 0, 2, lambda p: send.at[2, jnp.where(earlier(zh, p), 1, 0)])
        before_b, line = collect("seq_2", nz, 1, 0, bz, loc[1])
        bx = go("seq_1", nx, 1, 1, plain(4, line))
        more, plane = collect("seq_1", nx, 1, 1, bx, line)
        before_b += more
        by = go("seq_0", ny, 1, 2, plain(5, plane))
        more, _ = collect("seq_0", ny, 1, 2, by, plane)
        inc[1] = before_b + more
        _, whole = collect("seq_2", nz, 0, 2, az, before_a)
        inc[0] = whole

    def within_body(b, i, at, cols):
        within[b, i] = dot(sc[b, i], v[at, cols], NN)

    each_block(within_body)
    scan(0, False)

    for i in range(heads):
        loc[i] = jnp.zeros((DK, DK), f32)

    def forward_body(b, i, at, cols):
        prior16 = inc[i].astype(bf16)
        prior[b, i] = prior16
        inc[i] += st[b, i]
        mixed = within[b, i] + dot(q_ref[at, cols], prior16, NN)
        inverse = 1.0 / jnp.sqrt(jnp.mean(mixed * mixed, axis=-1, keepdims=True) + norm_eps)
        normed = mixed * inverse
        attn_ref[at, cols] = normed.astype(bf16)
        upstream = go_ref[at, cols].astype(f32)
        inner = jnp.mean(upstream * normed, axis=-1, keepdims=True)
        grad_mixed = ((upstream - normed * inner) * inverse).astype(bf16)
        gm[at, cols] = grad_mixed
        s = dot(q_ref[at, cols], grad_mixed, TN)
        gs[b, i] = s
        loc[i] += s

    each_block(forward_body)

    def backward_body(b, i, at, cols):
        grad_mixed = gm[at, cols]
        grad_scores = jnp.where(causal, dot(grad_mixed, v[at, cols], NT), 0.0).astype(bf16)
        grad_query = dot(grad_scores, k_ref[at, cols], NN) + dot(grad_mixed, prior[b, i], NT)
        gq_ref[at, cols] = grad_query.astype(bf16)
        gkp[b, i] = dot(grad_scores, q_ref[at, cols], TN)
        gvp[b, i] = dot(sc[b, i], grad_mixed, TN)

    each_block(backward_body)
    scan(1, True)

    @pl.loop(0, blocks)
    def _(step_back):
        b = blocks - 1 - step_back
        at = pl.ds(pl.multiple_of(b * BLOCK, BLOCK), BLOCK)
        for i in range(heads):
            cols = slice(i * DK, (i + 1) * DK)
            following16 = inc[i].astype(bf16)
            inc[i] += gs[b, i]
            grad_key = gkp[b, i] + dot(v[at, cols], following16, NT)
            gk_ref[at, cols] = grad_key.astype(bf16)
            grad_value = gvp[b, i] + dot(k_ref[at, cols], following16, NN)
            gvt[cols, at] = grad_value.T.astype(bf16)

    piece = nz * rows
    side = columns // 2

    @pl.loop(0, nl * 2)
    def _(h):
        term = dot(gvt[...], xg[h // 2, lax.rem(h, 2)], NN).astype(bf16)
        for t in range(feats // piece):
            p = h * (feats // piece) + t
            part = term[:, t * piece : (t + 1) * piece]
            pa[p] = part[:side]
            pb[lax.rem(p, nx) * ny + p // nx] = part[side:]

    a1 = exchange("seq_0", ny, lambda p: pa.at[pl.ds(p * nx, nx)], lambda kk: ra1.at[kk - 1], g_s.at[0], g_r.at[0])
    b1 = exchange("seq_1", nx, lambda p: pb.at[pl.ds(p * ny, ny)], lambda kk: rb1.at[kk - 1], g_s.at[1], g_r.at[1])
    sent += a1 + b1

    def summed_a(t):
        value = pa[yy * nx + t].astype(f32)
        for kk in range(ny - 1):
            value += ra1[kk, t].astype(f32)
        return value

    def summed_b(t):
        value = pb[xx * ny + t].astype(f32)
        for kk in range(nx - 1):
            value += rb1[kk, t].astype(f32)
        return value

    arrive(a1)

    @pl.loop(0, nx)
    def _(t):
        sa2[t] = summed_a(t).astype(bf16)

    a2 = exchange("seq_1", nx, lambda p: sa2.at[p], lambda kk: ra2.at[kk - 1], g_s.at[2], g_r.at[2])
    arrive(b1)

    @pl.loop(0, ny)
    def _(t):
        sb2[t] = summed_b(t).astype(bf16)

    b2 = exchange("seq_0", ny, lambda p: sb2.at[p], lambda kk: rb2.at[kk - 1], g_s.at[3], g_r.at[3])
    sent += a2 + b2
    final_a = summed_a(xx)
    arrive(a2)
    for kk in range(nx - 1):
        final_a += ra2[kk].astype(f32)
    tzf[:, :side] = final_a.T
    final_b = summed_b(yy)
    arrive(b2)
    for kk in range(ny - 1):
        final_b += rb2[kk].astype(f32)
    tzf[:, side:] = final_b.T
    tz[...] = tzf[...].astype(bf16)
    z3 = exchange(
        "seq_2", nz, lambda p: tz.at[pl.ds(pl.multiple_of(p * rows, rows), rows)], lambda kk: rz.at[kk - 1],
        g_s.at[4], g_r.at[4],
    )
    sent += z3
    result = tzf[pl.ds(pl.multiple_of(zh * rows, rows), rows)]
    arrive(z3)
    for kk in range(nz - 1):
        result += rz[kk].astype(f32)
    gl_ref[...] = result

    for copy in sent:
        copy.wait_send()

    @pl.loop(0, nl)
    def _(block):
        @pl.loop(0, CHUNKS)
        def _(j):
            side_copy(block, j, False).wait_send()

            @pl.when(jnp.logical_and(block <= zl, zl < nl - 1))
            def _():
                line_copy(block, j, True, False).wait_send()

            @pl.when(jnp.logical_and(block >= zl, zl > 0))
            def _():
                line_copy(block, j, False, False).wait_send()


def per_device(inputs, latent, queries, keys, grad_out):
    sizes = tuple(lax.axis_size(a) for a in (*SEQ, "head_0"))
    ny, nx, nz, nl = sizes
    tokens, feats = inputs.shape
    rows, columns = latent.shape
    heads, blocks = columns // DK, tokens // BLOCK
    seqs, everyone = ny * nx * nz, ny * nx * nz * rows
    side, piece = columns // 2, nz * rows
    dma = pltpu.SemaphoreType.DMA
    most = max(ny, nx, nz) - 1
    scratch = [
        pltpu.VMEM((seqs, rows // 2, columns), bf16),
        pltpu.VMEM((seqs, rows // 2, columns), bf16),
        pltpu.VMEM((everyone, columns), bf16),
        pltpu.VMEM((nl, 2, tokens, feats), bf16),
        pltpu.VMEM((tokens, columns), f32),
        pltpu.VMEM((tokens, columns), bf16),
        pltpu.VMEM((blocks, heads, BLOCK, BLOCK), bf16),
        pltpu.VMEM((blocks, heads, DK, DK), f32),
        pltpu.VMEM((blocks, heads, DK, DK), bf16),
        pltpu.VMEM((blocks, heads, BLOCK, DK), f32),
        pltpu.VMEM((tokens, columns), bf16),
        pltpu.VMEM((blocks, heads, DK, DK), f32),
        pltpu.VMEM((blocks, heads, BLOCK, DK), f32),
        pltpu.VMEM((blocks, heads, BLOCK, DK), f32),
        pltpu.VMEM((columns, tokens), bf16),
        pltpu.VMEM((heads, DK, DK), f32),
        pltpu.VMEM((2, 6, 2, DK, DK), bf16),
        pltpu.VMEM((2, 6, most, DK, DK), bf16),
        pltpu.VMEM((heads, DK, DK), f32),
        pltpu.VMEM((ny * nx, side, piece), bf16),
        pltpu.VMEM((ny * nx, side, piece), bf16),
        pltpu.VMEM((ny - 1, nx, side, piece), bf16),
        pltpu.VMEM((nx - 1, ny, side, piece), bf16),
        pltpu.VMEM((nx, side, piece), bf16),
        pltpu.VMEM((ny, side, piece), bf16),
        pltpu.VMEM((nx - 1, side, piece), bf16),
        pltpu.VMEM((ny - 1, side, piece), bf16),
        pltpu.VMEM((piece, columns), bf16),
        pltpu.VMEM((piece, columns), f32),
        pltpu.VMEM((nz - 1, rows, columns), bf16),
        dma,
        dma((2, most)), dma((2, most)),
        dma((2, most)), dma((2, most)),
        dma((2, most)), dma((2, most)),
        dma((nl, CHUNKS)), dma((nl, CHUNKS)), dma((nl, CHUNKS)),
        dma((nl, CHUNKS)), dma((nl, CHUNKS)),
        dma((2, 6, most)), dma((2, 6, most)),
        dma((5, most)), dma((5, most)),
    ]
    vmem = pl.BlockSpec(memory_space=pltpu.VMEM)
    like = jax.ShapeDtypeStruct(queries.shape, bf16)
    return pl.pallas_call(
        functools.partial(kernel, sizes),
        out_shape=(like, like, like, jax.ShapeDtypeStruct(latent.shape, f32)),
        in_specs=[vmem] * 5,
        out_specs=(vmem,) * 4,
        scratch_shapes=scratch,
        compiler_params=pltpu.CompilerParams(
            collective_id=0, has_side_effects=True, vmem_limit_bytes=56 << 20
        ),
    )(inputs, latent, queries, keys, grad_out)


def solution(mesh):
    torus = Mesh(mesh.devices.reshape(4, 4, 4, 4, 2), (*SEQ, *HEAD))
    placed = P(SEQ, HEAD)
    return jax.shard_map(
        per_device,
        mesh=torus,
        in_specs=(placed,) * 5,
        out_specs=(placed,) * 4,
        check_vma=False,
    )
```

time: 358 us -> 137 us (0.38)
  waiting for transfers between devices: 183 us -> 0 us
  Pallas kernels: 0 us -> 131 us
  blocking collectives: 94.5 us -> 0 us
  starting transfers between devices: 19.1 us -> 0 us
  local copies, waits for them, and re-layouts: 22 us -> 4.25 us
  matrix products: 14.8 us -> 0 us
  between operations: 14.4 us -> 0.65 us
  other arithmetic: 7.57 us -> 0 us
    all_gather x1 -> x0, waiting for transfers between devices: 133 us -> none  [per_device(): lax.all_gather(latent.astype(jnp.bfloat16), SEQ, axis=0, tiled=True)]
    pallas_call x0 -> x1, Pallas kernels: none -> 131 us  [per_device(): pl.pallas_call(functools.partial(kernel, sizes), out_shape=(like, like, l...]
    all_gather x6 -> x0, blocking collectives: 87.4 us -> none  [prefix_by_axis(): pieces = lax.all_gather(so_far.astype(jnp.bfloat16), axis)]
    all_to_all x3 -> x0, waiting for transfers between devices: 50.7 us -> none  [the longest x2 50.7 us: sum_at_owner(): lax.all_to_all(pieces, axis, split_axis=0, concat_axis=0, tiled=True)]
    all_to_all x3 -> x0, starting transfers between devices: 19 us -> none  [the longest x2 13.2 us: sum_at_owner(): lax.all_to_all(pieces, axis, split_axis=0, concat_axis=0, tiled=True)]
    dot_general x18 -> x0, matrix products: 14.8 us -> none  [the longest x1 4.2 us: per_device(): jnp.dot(features_all, ternarize(full_latent, column_scale), preferred_ele...]
    all_to_all x1 -> x0, blocking collectives: 7.1 us -> none  [from_everyone(): lax.all_to_all(jnp.broadcast_to(array[None], (count, *array.shape)), axis...]
    transpose x1 -> x0, local copies, waits for them, and re-layouts: 6.6 us -> none  [joined_along(): return jnp.moveaxis(pieces, 0, dim).reshape(lengths)]
  transfers between devices with their start and end apart: 4 -> 0, of which waited for: 3 -> 0; matrix products, arithmetic and copies ran while one was open for 3% -> 0% of each run, Pallas kernels for 0% -> 0%
where the time goes in v1:
time: 137 us; the launch traced here: 136 us
  Pallas kernels  131 us (96%)
  local copies, waits for them, and re-layouts  4.25 us (3%)
    pallas_call x1, Pallas kernels, per_device(): pl.pallas_call(functools.partial(kernel, sizes), out_shape=(like, like, l...  131 us
    unnamed x10, local copies, waits for them, and re-layouts  4.25 us

profile of v1, /device:TPU:6, one launch (start us, length us, event | category | flops | bytes accessed | tf_op | source)
XLA Modules:
  0.0 135.8 jit_solution(12004954688485398908)
XLA Ops:
  0.6 130.9 %shard_map.84 = (bf16[512,256]{1,0:T(8,128)(2,1)}, bf16[512,256]{1,0:T(8,128)(2,1)}, bf16[512,256]{1,0:T(8,128)(2,1)}, f32[64,256]{1,0:T(8,128)}) custom-call(bf16[512,512]{1,0:T(8,128)(2,1)} %x_ref.1, f32[64,256]{1,0:T(8,128)} %latent_ref.1, bf16[512,256]{1,0:T(8,128)(2,1)} %q_ref.1, bf16[512,256]{1,0:T(8,128)(2,1)} %k_ref.1, bf16[512,256]{1,0:T(8,128)(2,1)} %go_ref.1), custom_call_target="tpu_custom_call" | custom-call | tf_op jit(solution)/shard_map/pallas_call | solution.py:487
  131.5 0.0 copy-start.1
  131.5 1.7 %copy.13 = bf16[512,256]{1,0:T(8,128)(2,1)} copy(bf16[512,256]{1,0:T(8,128)(2,1)} %get-tuple-element.8) | data formatting | bytes 524288
  133.2 0.0 copy-done.1
  133.2 0.0 copy-start
  133.2 0.7 copy.14
  134.0 0.3 copy-done
  134.3 0.0 copy-start.2
  134.3 0.7 copy.15
  135.0 0.2 copy-done.2
  135.2 0.6 copy.16
Async XLA Ops:
  131.5 1.7 %copy-start.1 = (bf16[512,256]{1,0:T(8,128)(2,1)S(1)}, bf16[512,256]{1,0:T(8,128)(2,1)}, u32[]{:S(2)}) copy-start(bf16[512,256]{1,0:T(8,128)(2,1)} %get-tuple-element.9) | copy-start | bytes 786436
  133.2 1.0 copy-start
  134.3 0.9 copy-start.2

commit v2 on v1

v2 whole, which is shorter than its diff:
```python
import functools

import jax
import jax.numpy as jnp
from jax import lax
from jax.experimental import pallas as pl
from jax.experimental.pallas import tpu as pltpu
from jax.sharding import Mesh
from jax.sharding import PartitionSpec as P

DK = 128
BLOCK = 128
HEAD = ("head_0", "head_1")
SEQ = ("seq_0", "seq_1", "seq_2")
ID = pl.DeviceIdType.MESH
CHUNKS = 4

absmean_eps = 1e-05
norm_eps = 1e-06

f32 = jnp.float32
bf16 = jnp.bfloat16


def dot(a, b, contract):
    return lax.dot_general(a, b, ((contract[:1], contract[1:]), ((), ())), preferred_element_type=f32)


NN, NT, TN = (1, 0), (1, 1), (0, 0)


def exchange(axis, count, source, target, send, recv):
    position = lax.axis_index(axis)
    copies = []
    for kk in range(1, count):
        peer = lax.rem(position + kk, count)
        copy = pltpu.make_async_remote_copy(
            src_ref=source(peer),
            dst_ref=target(kk),
            send_sem=send.at[kk - 1],
            recv_sem=recv.at[kk - 1],
            device_id={axis: peer},
            device_id_type=ID,
        )
        copy.start()
        copies.append(copy)
    return copies


def arrive(copies):
    for copy in copies:
        copy.wait_recv()


def kernel(
    sizes, x_in, latent_in, q_in, k_in, go_in, attn_out, gq_out, gk_out, gl_out,
    attn_ref, gq_ref, gk_ref, gl_ref, latent_ref, q_ref, k_ref, go_ref, wa, wb, wt, xg, acc, v, sc, st, prior, within, gm, gs, following, gkp, gvp, gvt, loc, scan_send, scan_recv, zr, inc,
    pa, pb, ra1, rb1, sa2, sb2, ra2, rb2, tz, tzf, rz,
    own_sem, out_sem, wz_s, wz_r, w2_s, w2_r, w3_s, w3_r, xp_s, xm_s, xs_s, xl_r, xs_r, scan_s, scan_r, zs_s, zs_r, g1_s, g1_r, g_s, g_r,
):
    ny, nx, nz, nl = sizes
    yy, xx, zh = (lax.axis_index(a) for a in SEQ)
    zl, cc = (lax.axis_index(a) for a in HEAD)
    tokens, feats = x_in.shape
    rows, columns = latent_ref.shape
    half = rows // 2
    heads = columns // DK
    blocks = tokens // BLOCK
    step = tokens // CHUNKS
    sent = []

    written = [
        pltpu.make_async_copy(attn_ref, attn_out, out_sem.at[0]),
        pltpu.make_async_copy(gq_ref, gq_out, out_sem.at[1]),
        pltpu.make_async_copy(gk_ref, gk_out, out_sem.at[2]),
        pltpu.make_async_copy(gl_ref, gl_out, out_sem.at[3]),
    ]
    fetches = [
        pltpu.make_async_copy(latent_in, latent_ref, own_sem.at[0]),
        pltpu.make_async_copy(x_in, xg.at[zl, cc], own_sem.at[1]),
        pltpu.make_async_copy(q_in, q_ref, own_sem.at[2]),
        pltpu.make_async_copy(k_in, k_ref, own_sem.at[3]),
        pltpu.make_async_copy(go_in, go_ref, own_sem.at[4]),
    ]
    for fetch in fetches:
        fetch.start()
    at_a = (yy * nx + xx) * nz
    at_b = (xx * ny + yy) * nz
    barrier = pltpu.get_barrier_semaphore()
    for axis, count in (("seq_2", nz), ("seq_1", nx), ("seq_0", ny), ("head_1", 2)):
        position = lax.axis_index(axis)
        for kk in range(1, count):
            pl.semaphore_signal(
                barrier, inc=1, device_id={axis: lax.rem(position + kk, count)}, device_id_type=ID
            )

    @pl.when(zl > 0)
    def _():
        pl.semaphore_signal(barrier, inc=1, device_id={"head_0": zl - 1}, device_id_type=ID)

    @pl.when(zl < nl - 1)
    def _():
        pl.semaphore_signal(barrier, inc=1, device_id={"head_0": zl + 1}, device_id_type=ID)

    fetches[0].wait()
    latent16 = latent_ref[...].astype(bf16)
    wa[at_a + zh] = latent16[:half]
    wb[at_b + zh] = latent16[half:]
    fetches[1].wait()
    partners = (nz - 1) + (nx - 1) + (ny - 1) + 1
    neighbours = jnp.where(zl > 0, 1, 0) + jnp.where(zl < nl - 1, 1, 0)
    pl.semaphore_wait(barrier, partners + neighbours)

    up, down = lax.rem(zh + 1, nz), lax.rem(zh + nz - 1, nz)
    opposite = lax.rem(zh + 2, nz)

    def z_copy(peer, source, target, send, recv):
        copy = pltpu.make_async_remote_copy(
            src_ref=source, dst_ref=target, send_sem=send, recv_sem=recv,
            device_id={"seq_2": peer}, device_id_type=ID,
        )
        copy.start()
        sent.append(copy)
        return copy

    wz = exchange("seq_2", nz, lambda p: wa.at[at_a + zh], lambda kk: wa.at[at_a + zh], wz_s.at[0], wz_r.at[0])
    wz += exchange("seq_2", nz, lambda p: wb.at[at_b + zh], lambda kk: wb.at[at_b + zh], wz_s.at[1], wz_r.at[1])
    sent += wz

    def rows_of(ref, j):
        return ref.at[pl.ds(pl.multiple_of(j * step, step), step)]

    def line_copy(block, j, up):
        place = rows_of(xg.at[block, cc], j)
        return pltpu.make_async_remote_copy(
            src_ref=place,
            dst_ref=place,
            send_sem=(xp_s if up else xm_s).at[block, j],
            recv_sem=xl_r.at[block, j],
            device_id={"head_0": zl + 1 if up else zl - 1},
            device_id_type=ID,
        )

    def side_copy(block, j):
        place = rows_of(xg.at[block, cc], j)
        return pltpu.make_async_remote_copy(
            src_ref=place,
            dst_ref=place,
            send_sem=xs_s.at[block, j],
            recv_sem=xs_r.at[block, j],
            device_id={"head_1": 1 - cc},
            device_id_type=ID,
        )

    @pl.loop(0, CHUNKS)
    def _(j):
        @pl.when(zl < nl - 1)
        def _():
            line_copy(zl, j, True).start()

        @pl.when(zl > 0)
        def _():
            line_copy(zl, j, False).start()

    @pl.loop(0, CHUNKS)
    def _(j):
        side_copy(zl, j).start()

    def relay(distance):
        @pl.loop(0, CHUNKS)
        def _(j):
            @pl.when(zl >= distance)
            def _():
                block = zl - distance
                line_copy(block, j, True).wait_recv()

                @pl.when(zl < nl - 1)
                def _():
                    line_copy(block, j, True).start()

                side_copy(block, j).start()

            @pl.when(zl + distance < nl)
            def _():
                block = zl + distance
                line_copy(block, j, False).wait_recv()

                @pl.when(zl > 0)
                def _():
                    line_copy(block, j, False).start()

                side_copy(block, j).start()

    causal = lax.broadcasted_iota(jnp.int32, (BLOCK, BLOCK), 0) >= lax.broadcasted_iota(
        jnp.int32, (BLOCK, BLOCK), 1
    )

    def unrolled(body, first, last):
        for b in range(first, last):
            for i in range(heads):
                body(b, i, slice(b * BLOCK, (b + 1) * BLOCK), slice(i * DK, (i + 1) * DK))

    def each_block(body):
        @pl.loop(0, blocks)
        def _(b):
            at = pl.ds(pl.multiple_of(b * BLOCK, BLOCK), BLOCK)
            for i in range(heads):
                body(b, i, at, slice(i * DK, (i + 1) * DK))

    def scores_body(b, i, at, cols):
        s = dot(q_ref[at, cols], k_ref[at, cols], NT)
        sc[b, i] = jnp.where(causal, s, 0.0).astype(bf16)

    for fetch in fetches[2:]:
        fetch.wait()
    each_block(scores_body)

    arrive(wz)
    mine_a = wa.at[pl.ds(at_a, nz)]
    mine_b = wb.at[pl.ds(at_b, nz)]
    w2a = exchange("seq_1", nx, lambda p: mine_a, lambda kk: mine_a, w2_s.at[0], w2_r.at[0])
    w2b = exchange("seq_0", ny, lambda p: mine_b, lambda kk: mine_b, w2_s.at[1], w2_r.at[1])
    sent += w2a + w2b
    relay(1)
    row_a = wa.at[pl.ds(yy * nx * nz, nx * nz)]
    row_b = wb.at[pl.ds(xx * ny * nz, ny * nz)]
    arrive(w2a)
    w3a = exchange("seq_0", ny, lambda p: row_a, lambda kk: row_a, w3_s.at[0], w3_r.at[0])
    arrive(w2b)
    w3b = exchange("seq_1", nx, lambda p: row_b, lambda kk: row_b, w3_s.at[1], w3_r.at[1])
    sent += w3a + w3b
    for distance in range(2, nl - 1):
        relay(distance)
    arrive(w3a)
    arrive(w3b)

    def magnitude(s, total):
        both = jnp.abs(wa[s].astype(f32)) + jnp.abs(wb[s].astype(f32))
        return total + both.reshape(half // 8, 8, columns).sum(axis=0)

    total = lax.fori_loop(0, ny * nx * nz, magnitude, jnp.zeros((8, columns), f32))
    scale = total.sum(axis=0, keepdims=True) / (ny * nx * nz * rows) + absmean_eps
    halfway = 0.5 * scale

    def ternary(w):
        w = w.astype(f32)
        return jnp.where(w > halfway, scale, jnp.where(w < -halfway, -scale, 0.0)).astype(bf16)

    @pl.loop(0, ny * nx)
    def _(p):
        other = lax.rem(p, nx) * ny + p // nx
        for z in range(nz):
            at = pl.multiple_of((p * nz + z) * rows, rows)
            wt[pl.ds(at, half)] = ternary(wa[p * nz + z])
            wt[pl.ds(pl.multiple_of(at + half, half), half)] = ternary(wb[other * nz + z])

    acc[...] = jnp.zeros_like(acc)

    def features(block, core):
        return wt[pl.ds(pl.multiple_of((block * 2 + core) * feats, feats), feats)]

    @pl.loop(0, nl)
    def _(block):
        @pl.when(jnp.abs(block - zl) < nl - 1)
        def _():
            @pl.loop(0, CHUNKS)
            def _(j):
                side_copy(block, j).wait_recv()

            @pl.loop(0, 2)
            def _(core):
                acc[...] += dot(xg[block, core], features(block, core), NN)

    @pl.when(jnp.logical_or(zl == 0, zl == nl - 1))
    def _():
        far = nl - 1 - zl

        @pl.loop(0, CHUNKS)
        def _(j):
            at = pl.ds(pl.multiple_of(j * step, step), step)
            line_copy(far, j, True).wait_recv()
            side_copy(far, j).start()
            acc[at] += dot(xg[far, cc, at], features(far, cc), NN)
            side_copy(far, j).wait_recv()
            acc[at] += dot(xg[far, 1 - cc, at], features(far, 1 - cc), NN)

    v[...] = acc[...].astype(bf16)

    totals = [jnp.zeros((DK, DK), f32)] * heads

    def state_body(b, i, at, cols):
        s = dot(k_ref[at, cols], v[at, cols], TN)
        st[b, i] = s
        totals[i] = totals[i] + s

    unrolled(state_body, 0, blocks)
    for i in range(heads):
        loc[i] = totals[i]

    def scan(which, reverse, works):
        def earlier(p, mine):
            return p > mine if reverse else p < mine

        send, recv = scan_send.at[which], scan_recv.at[which]

        def go(axis, count, i, stage, source):
            slot = i * 3 + stage
            copies = exchange(
                axis, count, source, lambda kk: recv.at[slot, kk - 1],
                scan_s.at[which, slot], scan_r.at[which, slot],
            )
            sent.extend(copies)
            return copies

        def collect(axis, count, i, stage, copies, mine):
            position = lax.axis_index(axis)
            before, everything = jnp.zeros((DK, DK), f32), mine
            for kk in range(1, count):
                copies[kk - 1].wait_recv()
                value = recv[i * 3 + stage, kk - 1].astype(f32)
                sender = lax.rem(position + count - kk, count)
                before += jnp.where(earlier(sender, position), value, 0.0)
                everything += value
            return before, everything

        def plain(slot, value):
            send[slot, 0] = value.astype(bf16)
            return lambda p: send.at[slot, 0]

        top, bottom = pl.ds(0, DK // 2), pl.ds(DK // 2, DK // 2)

        def step_z(peer, source, target, n):
            return z_copy(peer, source, target, zs_s.at[which, n], zs_r.at[which, n])

        ax = go("seq_1", nx, 0, 0, plain(0, loc[0]))
        send[3, 0] = loc[1].astype(bf16)
        from_z = zr.at[which, 0]
        bz = [
            step_z(up, send.at[3, 0], from_z.at[0], 0),
            step_z(down, send.at[3, 0], from_z.at[1], 1),
            step_z(opposite, send.at[3, 0], from_z.at[2], 2),
        ]
        works[0]()
        before_a, row = collect("seq_1", nx, 0, 0, ax, loc[0])
        ay = go("seq_0", ny, 0, 1, plain(1, row))
        works[1]()
        more, _ = collect("seq_0", ny, 0, 1, ay, row)
        before_a += more
        send[2, 0] = before_a.astype(bf16)
        send[2, 1] = (before_a + loc[0]).astype(bf16)

        def message(peer):
            return send.at[2, jnp.where(earlier(zh, peer), 1, 0)]

        to_z = zr.at[which, 1]
        az = [
            step_z(up, message(opposite).at[top], to_z.at[2, top], 4),
            step_z(down, message(opposite).at[bottom], to_z.at[2, bottom], 5),
            step_z(up, message(up).at[bottom], to_z.at[0, bottom], 6),
            step_z(down, message(down).at[top], to_z.at[1, top], 7),
        ]
        before_b, line = jnp.zeros((DK, DK), f32), loc[1]
        arrive(bz)
        for n, sender in ((0, down), (1, up), (2, opposite)):
            value = from_z[n].astype(f32)
            before_b += jnp.where(earlier(sender, zh), value, 0.0)
            line += value
        bx = go("seq_1", nx, 1, 1, plain(4, line))
        half_rows = DK // 2
        az[0].wait_recv()
        send[5, 1, :half_rows] = (to_z[2, :half_rows].astype(f32) + message(up)[:half_rows].astype(f32)).astype(bf16)
        az += [step_z(up, send.at[5, 1, top], to_z.at[0, top], 8)]
        az[1].wait_recv()
        send[5, 1, half_rows:] = (to_z[2, half_rows:].astype(f32) + message(down)[half_rows:].astype(f32)).astype(bf16)
        az += [step_z(down, send.at[5, 1, bottom], to_z.at[1, bottom], 9)]
        more, plane = collect("seq_1", nx, 1, 1, bx, line)
        before_b += more
        by = go("seq_0", ny, 1, 2, plain(5, plane))
        more, _ = collect("seq_0", ny, 1, 2, by, plane)
        inc[1] = before_b + more
        arrive(az[2:])
        inc[0] = before_a + to_z[0].astype(f32) + to_z[1].astype(f32)

    def within_body(b, i, at, cols):
        within[b, i] = dot(sc[b, i], v[at, cols], NN)

    halfway_block = blocks // 2
    scan(
        0, False,
        (lambda: unrolled(within_body, 0, halfway_block), lambda: unrolled(within_body, halfway_block, blocks)),
    )

    for i in range(heads):
        loc[i] = jnp.zeros((DK, DK), f32)

    def forward_body(b, i, at, cols):
        prior16 = inc[i].astype(bf16)
        prior[b, i] = prior16
        inc[i] += st[b, i]
        mixed = within[b, i] + dot(q_ref[at, cols], prior16, NN)
        inverse = 1.0 / jnp.sqrt(jnp.mean(mixed * mixed, axis=-1, keepdims=True) + norm_eps)
        normed = mixed * inverse
        attn_ref[at, cols] = normed.astype(bf16)
        upstream = go_ref[at, cols].astype(f32)
        inner = jnp.mean(upstream * normed, axis=-1, keepdims=True)
        grad_mixed = ((upstream - normed * inner) * inverse).astype(bf16)
        gm[at, cols] = grad_mixed
        s = dot(q_ref[at, cols], grad_mixed, TN)
        gs[b, i] = s
        loc[i] += s

    each_block(forward_body)
    written[0].start()

    def backward_body(b, i, at, cols):
        grad_mixed = gm[at, cols]
        grad_scores = jnp.where(causal, dot(grad_mixed, v[at, cols], NT), 0.0).astype(bf16)
        grad_query = dot(grad_scores, k_ref[at, cols], NN) + dot(grad_mixed, prior[b, i], NT)
        gq_ref[at, cols] = grad_query.astype(bf16)
        gkp[b, i] = dot(grad_scores, q_ref[at, cols], TN)
        gvp[b, i] = dot(sc[b, i], grad_mixed, TN)

    scan(
        1, True,
        (lambda: unrolled(backward_body, 0, halfway_block), lambda: unrolled(backward_body, halfway_block, blocks)),
    )

    written[1].start()
    carried = [inc[i] for i in range(heads)]
    for b in reversed(range(blocks)):
        at = slice(b * BLOCK, (b + 1) * BLOCK)
        for i in range(heads):
            cols = slice(i * DK, (i + 1) * DK)
            following16 = carried[i].astype(bf16)
            following[b, i] = following16
            carried[i] = carried[i] + gs[b, i]
            grad_value = gvp[b, i] + dot(k_ref[at, cols], following16, NN)
            gvt[cols, at] = grad_value.T.astype(bf16)

    piece = nz * rows
    side = columns // 2

    per_block = feats // piece
    order = []
    for k in (2, 1, 3, 0):
        order += [(dy, k) for dy in (2, 1, 3, 0)] + [(k, dx) for dx in (2, 1, 3, 0)]
    half_side = side // 2
    first, second_half = slice(0, half_side), slice(half_side, side)
    ring = {}

    def hop(which, k, n, forward, source, target):
        axis, position, count = (("seq_0", yy, ny), ("seq_1", xx, nx))[which]
        peer = lax.rem(position + (1 if forward else count - 1), count)
        copy = pltpu.make_async_remote_copy(
            src_ref=source, dst_ref=target,
            send_sem=g1_s.at[which, k, n], recv_sem=g1_r.at[which, k, n],
            device_id={axis: peer}, device_id_type=ID,
        )
        copy.start()
        sent.append(copy)
        ring[which, k, n] = copy

    def begin(which, distance, k, source, target):
        if distance == 2:
            hop(which, k, 0, True, source.at[first], target.at[2, k, first])
            hop(which, k, 1, False, source.at[second_half], target.at[2, k, second_half])
        elif distance == 1:
            hop(which, k, 2, True, source.at[second_half], target.at[0, k, second_half])
        elif distance == 3:
            hop(which, k, 3, False, source.at[first], target.at[1, k, first])

    def pass_on(which, k, ahead, behind, target):
        ring[which, k, 0].wait_recv()
        ahead[first] = (ahead[first].astype(f32) + target[2, k, first].astype(f32)).astype(bf16)
        hop(which, k, 4, True, ahead.at[first], target.at[0, k, first])
        ring[which, k, 1].wait_recv()
        behind[second_half] = (behind[second_half].astype(f32) + target[2, k, second_half].astype(f32)).astype(bf16)
        hop(which, k, 5, False, behind.at[second_half], target.at[1, k, second_half])

    def pass_both(k):
        pass_on(0, k, pa.at[1, k], pa.at[3, k], ra1)
        pass_on(1, k, pb.at[k, 1], pb.at[k, 3], rb1)

    for n, (dy, dx) in enumerate(dict.fromkeys(order)):
        to_y, to_x = lax.rem(yy + dy, ny), lax.rem(xx + dx, nx)
        p = to_y * nx + to_x
        block = p // per_block
        lanes = pl.ds(pl.multiple_of(lax.rem(p, per_block) * piece, piece), piece)
        term = dot(gvt[...], xg[block // 2, lax.rem(block, 2), :, lanes], NN).astype(bf16)
        pa[dy, dx] = term[:side]
        pb[dy, dx] = term[side:]
        begin(0, dy, dx, pa.at[dy, dx], ra1)
        begin(1, dx, dy, pb.at[dy, dx], rb1)
        if n == 11:
            pass_both(2)
    for k in (1, 3, 0):
        pass_both(k)

    def key_body(b, i, at, cols):
        grad_key = gkp[b, i] + dot(v[at, cols], following[b, i], NT)
        gk_ref[at, cols] = grad_key.astype(bf16)

    each_block(key_body)
    written[2].start()

    def summed_a(dx):
        value = pa[0, dx].astype(f32)
        for n in (2, 3, 4, 5):
            ring[0, dx, n].wait_recv()
        return value + ra1[0, dx].astype(f32) + ra1[1, dx].astype(f32)

    def summed_b(dy):
        value = pb[dy, 0].astype(f32)
        for n in (2, 3, 4, 5):
            ring[1, dy, n].wait_recv()
        return value + rb1[0, dy].astype(f32) + rb1[1, dy].astype(f32)

    def second(axis, position, count, k, source, target, which):
        copy = pltpu.make_async_remote_copy(
            src_ref=source.at[k - 1], dst_ref=target.at[k - 1],
            send_sem=g_s.at[which, k - 1], recv_sem=g_r.at[which, k - 1],
            device_id={axis: lax.rem(position + k, count)}, device_id_type=ID,
        )
        copy.start()
        sent.append(copy)
        return copy

    a2, b2 = [], []
    for k in (2, 1, 3):
        if k < nx:
            sa2[k - 1] = summed_a(k).astype(bf16)
            a2.append(second("seq_1", xx, nx, k, sa2, ra2, 0))
        if k < ny:
            sb2[k - 1] = summed_b(k).astype(bf16)
            b2.append(second("seq_0", yy, ny, k, sb2, rb2, 1))
    final_a, final_b = summed_a(0), summed_b(0)

    def last(final, second_copies, received, which):
        for copy in second_copies:
            copy.wait_recv()
        for kk in range(len(second_copies)):
            final += received[kk].astype(f32)
        final = final.T
        tzf[which] = final
        tz[which] = final.astype(bf16)
        return exchange(
            "seq_2", nz, lambda p: tz.at[which, pl.ds(pl.multiple_of(p * rows, rows), rows)],
            lambda kk: rz.at[which, kk - 1], g_s.at[2 + which], g_r.at[2 + which],
        )

    z3 = [last(final_a, a2, ra2, 0), last(final_b, b2, rb2, 1)]
    for which, copies in enumerate(z3):
        sent += copies
        result = tzf[which, pl.ds(pl.multiple_of(zh * rows, rows), rows)]
        arrive(copies)
        for kk in range(nz - 1):
            result += rz[which, kk].astype(f32)
        gl_ref[:, which * side : (which + 1) * side] = result

    written[3].start()
    for copy in sent:
        copy.wait_send()
    for copy in written:
        copy.wait()

    @pl.loop(0, nl)
    def _(block):
        @pl.loop(0, CHUNKS)
        def _(j):
            side_copy(block, j).wait_send()

            @pl.when(jnp.logical_and(block <= zl, zl < nl - 1))
            def _():
                line_copy(block, j, True).wait_send()

            @pl.when(jnp.logical_and(block >= zl, zl > 0))
            def _():
                line_copy(block, j, False).wait_send()


def deliver(*refs):
    sems = refs[12]
    inward = [pltpu.make_async_copy(refs[i], refs[8 + i], sems.at[0, i]) for i in range(4)]
    outward = [pltpu.make_async_copy(refs[8 + i], refs[4 + i], sems.at[1, i]) for i in range(4)]
    for copy in inward:
        copy.start()
    for copy, following in zip(inward, outward):
        copy.wait()
        following.start()
    for copy in outward:
        copy.wait()


def per_device(inputs, latent, queries, keys, grad_out):
    sizes = tuple(lax.axis_size(a) for a in (*SEQ, "head_0"))
    ny, nx, nz, nl = sizes
    tokens, feats = inputs.shape
    rows, columns = latent.shape
    heads, blocks = columns // DK, tokens // BLOCK
    seqs, everyone = ny * nx * nz, ny * nx * nz * rows
    side, piece = columns // 2, nz * rows
    dma = pltpu.SemaphoreType.DMA
    most = max(ny, nx, nz) - 1
    scratch = [
        *[pltpu.VMEM((tokens, columns), bf16)] * 3,
        pltpu.VMEM(latent.shape, f32),
        pltpu.VMEM(latent.shape, f32),
        pltpu.VMEM((tokens, columns), bf16),
        pltpu.VMEM((tokens, columns), bf16),
        pltpu.VMEM((tokens, columns), bf16),
        pltpu.VMEM((seqs, rows // 2, columns), bf16),
        pltpu.VMEM((seqs, rows // 2, columns), bf16),
        pltpu.VMEM((everyone, columns), bf16),
        pltpu.VMEM((nl, 2, tokens, feats), bf16),
        pltpu.VMEM((tokens, columns), f32),
        pltpu.VMEM((tokens, columns), bf16),
        pltpu.VMEM((blocks, heads, BLOCK, BLOCK), bf16),
        pltpu.VMEM((blocks, heads, DK, DK), f32),
        pltpu.VMEM((blocks, heads, DK, DK), bf16),
        pltpu.VMEM((blocks, heads, BLOCK, DK), f32),
        pltpu.VMEM((tokens, columns), bf16),
        pltpu.VMEM((blocks, heads, DK, DK), f32),
        pltpu.VMEM((blocks, heads, DK, DK), bf16),
        pltpu.VMEM((blocks, heads, BLOCK, DK), f32),
        pltpu.VMEM((blocks, heads, BLOCK, DK), f32),
        pltpu.VMEM((columns, tokens), bf16),
        pltpu.VMEM((heads, DK, DK), f32),
        pltpu.VMEM((2, 6, 2, DK, DK), bf16),
        pltpu.VMEM((2, 6, most, DK, DK), bf16),
        pltpu.VMEM((2, 2, 3, DK, DK), bf16),
        pltpu.VMEM((heads, DK, DK), f32),
        pltpu.VMEM((ny, nx, side, piece), bf16),
        pltpu.VMEM((ny, nx, side, piece), bf16),
        pltpu.VMEM((ny - 1, nx, side, piece), bf16),
        pltpu.VMEM((nx - 1, ny, side, piece), bf16),
        pltpu.VMEM((nx - 1, side, piece), bf16),
        pltpu.VMEM((ny - 1, side, piece), bf16),
        pltpu.VMEM((nx - 1, side, piece), bf16),
        pltpu.VMEM((ny - 1, side, piece), bf16),
        pltpu.VMEM((2, piece, side), bf16),
        pltpu.VMEM((2, piece, side), f32),
        pltpu.VMEM((2, nz - 1, rows, side), bf16),
        dma((5,)),
        dma((4,)),
        dma((2, most)), dma((2, most)),
        dma((2, most)), dma((2, most)),
        dma((2, most)), dma((2, most)),
        dma((nl, CHUNKS)), dma((nl, CHUNKS)), dma((nl, CHUNKS)),
        dma((nl, CHUNKS)), dma((nl, CHUNKS)),
        dma((2, 6, most)), dma((2, 6, most)),
        dma((2, 10)), dma((2, 10)),
        dma((2, 4, 6)), dma((2, 4, 6)),
        dma((4, most)), dma((4, most)),
    ]
    like = jax.ShapeDtypeStruct(queries.shape, bf16)
    results = pl.pallas_call(
        functools.partial(kernel, sizes),
        out_shape=(like, like, like, jax.ShapeDtypeStruct(latent.shape, f32)),
        in_specs=[pl.BlockSpec(memory_space=pltpu.HBM)] * 5,
        out_specs=(pl.BlockSpec(memory_space=pltpu.HBM),) * 4,
        scratch_shapes=scratch,
        compiler_params=pltpu.CompilerParams(
            collective_id=0, has_side_effects=True, vmem_limit_bytes=60 << 20
        ),
    )(inputs, latent, queries, keys, grad_out)
    return pl.pallas_call(
        deliver,
        out_shape=(like, like, like, jax.ShapeDtypeStruct(latent.shape, f32)),
        in_specs=[pl.BlockSpec(memory_space=pltpu.HBM)] * 4,
        out_specs=(pl.BlockSpec(memory_space=pltpu.HBM),) * 4,
        scratch_shapes=[
            *[pltpu.VMEM(queries.shape, bf16)] * 3,
            pltpu.VMEM(latent.shape, f32),
            pltpu.SemaphoreType.DMA((2, 4)),
        ],
        compiler_params=pltpu.CompilerParams(vmem_limit_bytes=60 << 20),
    )(*results)


def solution(mesh):
    torus = Mesh(mesh.devices.reshape(4, 4, 4, 4, 2), (*SEQ, *HEAD))
    placed = P(SEQ, HEAD)
    return jax.shard_map(
        per_device,
        mesh=torus,
        in_specs=(placed,) * 5,
        out_specs=(placed,) * 4,
        check_vma=False,
    )
```

time: 137 us -> 126 us (0.920)
  Pallas kernels: 131 us -> 124 us
  local copies, waits for them, and re-layouts: 4.25 us -> 0 us
    pallas_call x1, Pallas kernels: 131 us -> 122 us  [per_device(): pl.pallas_call(functools.partial(kernel, sizes), out_shape=(like, like, l...]
    unnamed x10 -> x0, local copies, waits for them, and re-layouts: 4.25 us -> none
    pallas_call x0 -> x1, Pallas kernels: none -> 1.91 us  [per_device(): pl.pallas_call(deliver, out_shape=(like, like, like, jax.ShapeDtypeStruct...]
where the time goes in v2:
time: 126 us; the launch traced here: 125 us
  Pallas kernels  124 us (98%)
    pallas_call x1, Pallas kernels, per_device(): pl.pallas_call(functools.partial(kernel, sizes), out_shape=(like, like, l...  122 us

profile of v2, /device:TPU:6, one launch (start us, length us, event | category | flops | bytes accessed | tf_op | source)
XLA Modules:
  0.0 124.9 jit_solution(6129634538156518556)
XLA Ops:
  0.6 122.3 %shard_map.84 = (bf16[512,256]{1,0:T(8,128)(2,1)}, bf16[512,256]{1,0:T(8,128)(2,1)}, bf16[512,256]{1,0:T(8,128)(2,1)}, f32[64,256]{1,0:T(8,128)}) custom-call(bf16[512,512]{1,0:T(8,128)(2,1)} %x_in.1, f32[64,256]{1,0:T(8,128)} %latent_in.1, bf16[512,256]{1,0:T(8,128)(2,1)} %q_in.1, bf16[512,256]{1,0:T(8,128)(2,1)} %k_in.1, bf16[512,256]{1,0:T(8,128)(2,1)} %go_in.1), custom_call_target="tpu_custom_call" | custom-call | tf_op jit(solution)/shard_map/pallas_call | solution.py:656
  123.0 1.9 %shard_map.85 = (bf16[512,256]{1,0:T(8,128)(2,1)}, bf16[512,256]{1,0:T(8,128)(2,1)}, bf16[512,256]{1,0:T(8,128)(2,1)}, f32[64,256]{1,0:T(8,128)}) custom-call(bf16[512,256]{1,0:T(8,128)(2,1)} %get-tuple-element.8.refs_0_, bf16[512,256]{1,0:T(8,128)(2,1)} %get-tuple-element.9.refs_1_, bf16[512,256]{1,0:T(8,128)(2,1)} %get-tuple-element.10.refs_2_, ...), custom_call_target="tpu_custom_call" | custom-call | tf_op jit(solution)/shard_map/pallas_call | solution.py:666

commit v3 on v2

--- a/solution.py
+++ b/solution.py
@@ -1,4 +1,5 @@
 import functools
+import itertools
 
 import jax
 import jax.numpy as jnp
@@ -13,7 +14,8 @@
 HEAD = ("head_0", "head_1")
 SEQ = ("seq_0", "seq_1", "seq_2")
 ID = pl.DeviceIdType.MESH
-CHUNKS = 4
+CHUNKS = 8
+EARLY = 3
 
 absmean_eps = 1e-05
 norm_eps = 1e-06
@@ -53,10 +55,10 @@
 
 
 def kernel(
-    sizes, x_in, latent_in, q_in, k_in, go_in, attn_out, gq_out, gk_out, gl_out,
-    attn_ref, gq_ref, gk_ref, gl_ref, latent_ref, q_ref, k_ref, go_ref, wa, wb, wt, xg, acc, v, sc, st, prior, within, gm, gs, following, gkp, gvp, gvt, loc, scan_send, scan_recv, zr, inc,
+    sizes, x_in, latent_in, q_in, k_in, go_in, attn_ref, gq_ref, gk_ref, gl_ref,
+    latent_ref, q_ref, k_ref, go_ref, wa, wb, wt, xg, acc, v, sc, st, prior, within, gm, gs, following, gkp, gvp, gvt, loc, scan_send, scan_recv, zr, inc,
     pa, pb, ra1, rb1, sa2, sb2, ra2, rb2, tz, tzf, rz,
-    own_sem, out_sem, wz_s, wz_r, w2_s, w2_r, w3_s, w3_r, xp_s, xm_s, xs_s, xl_r, xs_r, scan_s, scan_r, zs_s, zs_r, g1_s, g1_r, g_s, g_r,
+    own_sem, wz_s, wz_r, w2_s, w2_r, w3_s, w3_r, xp_s, xm_s, xs_s, xl_r, xs_r, scan_s, scan_r, zs_s, zs_r, g1_s, g1_r, g_s, g_r,
 ):
     ny, nx, nz, nl = sizes
     yy, xx, zh = (lax.axis_index(a) for a in SEQ)
@@ -69,12 +71,6 @@
     step = tokens // CHUNKS
     sent = []
 
-    written = [
-        pltpu.make_async_copy(attn_ref, attn_out, out_sem.at[0]),
-        pltpu.make_async_copy(gq_ref, gq_out, out_sem.at[1]),
-        pltpu.make_async_copy(gk_ref, gk_out, out_sem.at[2]),
-        pltpu.make_async_copy(gl_ref, gl_out, out_sem.at[3]),
-    ]
     fetches = [
         pltpu.make_async_copy(latent_in, latent_ref, own_sem.at[0]),
         pltpu.make_async_copy(x_in, xg.at[zl, cc], own_sem.at[1]),
@@ -123,9 +119,15 @@
         sent.append(copy)
         return copy
 
-    wz = exchange("seq_2", nz, lambda p: wa.at[at_a + zh], lambda kk: wa.at[at_a + zh], wz_s.at[0], wz_r.at[0])
-    wz += exchange("seq_2", nz, lambda p: wb.at[at_b + zh], lambda kk: wb.at[at_b + zh], wz_s.at[1], wz_r.at[1])
-    sent += wz
+    def w_copy(peer, ref, at, n):
+        return z_copy(peer, ref.at[at], ref.at[at], wz_s.at[n], wz_r.at[n])
+
+    wz = [
+        w_copy(up, wa, at_a + zh, 0),
+        w_copy(down, wb, at_b + zh, 1),
+        w_copy(up, wb, at_b + zh, 2),
+        w_copy(down, wa, at_a + zh, 3),
+    ]
 
     def rows_of(ref, j):
         return ref.at[pl.ds(pl.multiple_of(j * step, step), step)]
@@ -152,22 +154,23 @@
             device_id_type=ID,
         )
 
-    @pl.loop(0, CHUNKS)
-    def _(j):
-        @pl.when(zl < nl - 1)
-        def _():
-            line_copy(zl, j, True).start()
-
-        @pl.when(zl > 0)
-        def _():
-            line_copy(zl, j, False).start()
-
-    @pl.loop(0, CHUNKS)
-    def _(j):
-        side_copy(zl, j).start()
-
-    def relay(distance):
-        @pl.loop(0, CHUNKS)
+    def send_own(first, last):
+        @pl.loop(first, last)
+        def _(j):
+            @pl.when(zl < nl - 1)
+            def _():
+                line_copy(zl, j, True).start()
+
+            @pl.when(zl > 0)
+            def _():
+                line_copy(zl, j, False).start()
+
+            side_copy(zl, j).start()
+
+    send_own(0, EARLY)
+
+    def relay(distance, first, last):
+        @pl.loop(first, last)
         def _(j):
             @pl.when(zl >= distance)
             def _():
@@ -215,13 +218,19 @@
         fetch.wait()
     each_block(scores_body)
 
-    arrive(wz)
+    wz[0].wait_recv()
+    wz += [w_copy(up, wa, at_a + down, 4)]
+    wz[1].wait_recv()
+    wz += [w_copy(down, wb, at_b + up, 5)]
+    send_own(EARLY, CHUNKS)
+    relay(1, 0, CHUNKS // 2)
+    arrive(wz[2:])
     mine_a = wa.at[pl.ds(at_a, nz)]
     mine_b = wb.at[pl.ds(at_b, nz)]
     w2a = exchange("seq_1", nx, lambda p: mine_a, lambda kk: mine_a, w2_s.at[0], w2_r.at[0])
     w2b = exchange("seq_0", ny, lambda p: mine_b, lambda kk: mine_b, w2_s.at[1], w2_r.at[1])
     sent += w2a + w2b
-    relay(1)
+    relay(1, CHUNKS // 2, CHUNKS)
     row_a = wa.at[pl.ds(yy * nx * nz, nx * nz)]
     row_b = wb.at[pl.ds(xx * ny * nz, ny * nz)]
     arrive(w2a)
@@ -230,9 +239,23 @@
     w3b = exchange("seq_1", nx, lambda p: row_b, lambda kk: row_b, w3_s.at[1], w3_r.at[1])
     sent += w3a + w3b
     for distance in range(2, nl - 1):
-        relay(distance)
+        relay(distance, 0, CHUNKS)
     arrive(w3a)
     arrive(w3b)
+    far = nl - 1 - zl
+
+    def at_end(body):
+        pl.when(jnp.logical_or(zl == 0, zl == nl - 1))(body)
+
+    def share_far(first, last):
+        @at_end
+        def _():
+            @pl.loop(first, last)
+            def _(j):
+                line_copy(far, j, True).wait_recv()
+                side_copy(far, j).start()
+
+    share_far(0, 2)
 
     def magnitude(s, total):
         both = jnp.abs(wa[s].astype(f32)) + jnp.abs(wb[s].astype(f32))
@@ -254,6 +277,7 @@
             wt[pl.ds(at, half)] = ternary(wa[p * nz + z])
             wt[pl.ds(pl.multiple_of(at + half, half), half)] = ternary(wb[other * nz + z])
 
+    share_far(2, 3)
     acc[...] = jnp.zeros_like(acc)
 
     def features(block, core):
@@ -271,18 +295,32 @@
             def _(core):
                 acc[...] += dot(xg[block, core], features(block, core), NN)
 
-    @pl.when(jnp.logical_or(zl == 0, zl == nl - 1))
+    share_far(3, CHUNKS // 2 + 1)
+
+    @at_end
     def _():
-        far = nl - 1 - zl
-
-        @pl.loop(0, CHUNKS)
+        half_at = pl.ds(0, tokens // 2)
+
+        @pl.loop(0, CHUNKS // 2)
         def _(j):
-            at = pl.ds(pl.multiple_of(j * step, step), step)
-            line_copy(far, j, True).wait_recv()
-            side_copy(far, j).start()
-            acc[at] += dot(xg[far, cc, at], features(far, cc), NN)
             side_copy(far, j).wait_recv()
-            acc[at] += dot(xg[far, 1 - cc, at], features(far, 1 - cc), NN)
+
+        acc[half_at] += dot(xg[far, cc, half_at], features(far, cc), NN)
+        acc[half_at] += dot(xg[far, 1 - cc, half_at], features(far, 1 - cc), NN)
+
+        def multiply(core, j):
+            at = slice(j * step, (j + 1) * step)
+            acc[at] += dot(xg[far, core, at], features(far, core), NN)
+
+        for j in range(CHUNKS // 2, CHUNKS):
+            if j > CHUNKS // 2:
+                line_copy(far, j, True).wait_recv()
+                side_copy(far, j).start()
+                side_copy(far, j - 1).wait_recv()
+                multiply(1 - cc, j - 1)
+            multiply(cc, j)
+        side_copy(far, CHUNKS - 1).wait_recv()
+        multiply(1 - cc, CHUNKS - 1)
 
     v[...] = acc[...].astype(bf16)
 
@@ -297,120 +335,150 @@
     for i in range(heads):
         loc[i] = totals[i]
 
-    def scan(which, reverse, works):
-        def earlier(p, mine):
-            return p > mine if reverse else p < mine
-
-        send, recv = scan_send.at[which], scan_recv.at[which]
-
-        def go(axis, count, i, stage, source):
-            slot = i * 3 + stage
-            copies = exchange(
-                axis, count, source, lambda kk: recv.at[slot, kk - 1],
-                scan_s.at[which, slot], scan_r.at[which, slot],
-            )
-            sent.extend(copies)
-            return copies
-
-        def collect(axis, count, i, stage, copies, mine):
-            position = lax.axis_index(axis)
-            before, everything = jnp.zeros((DK, DK), f32), mine
-            for kk in range(1, count):
-                copies[kk - 1].wait_recv()
-                value = recv[i * 3 + stage, kk - 1].astype(f32)
-                sender = lax.rem(position + count - kk, count)
-                before += jnp.where(earlier(sender, position), value, 0.0)
-                everything += value
-            return before, everything
-
-        def plain(slot, value):
-            send[slot, 0] = value.astype(bf16)
-            return lambda p: send.at[slot, 0]
-
-        top, bottom = pl.ds(0, DK // 2), pl.ds(DK // 2, DK // 2)
-
-        def step_z(peer, source, target, n):
-            return z_copy(peer, source, target, zs_s.at[which, n], zs_r.at[which, n])
-
-        ax = go("seq_1", nx, 0, 0, plain(0, loc[0]))
-        send[3, 0] = loc[1].astype(bf16)
-        from_z = zr.at[which, 0]
+    part = DK // 2
+    tasks, serial = [], itertools.count()
+    finished = {}
+
+    def exchange_part(axis, count, which, i, r, stage, slot):
+        copies = exchange(
+            axis, count, lambda p: scan_send.at[which, i, r, slot], lambda kk: scan_recv.at[which, i, r, stage, kk - 1],
+            scan_s.at[which, i, r, stage], scan_r.at[which, i, r, stage],
+        )
+        sent.extend(copies)
+        return copies
+
+    def collect(axis, count, which, i, r, stage, copies, mine):
+        position = lax.axis_index(axis)
+        before, everything = jnp.zeros((part, DK), f32), mine
+        for kk in range(1, count):
+            copies[kk - 1].wait_recv()
+            value = scan_recv[which, i, r, stage, kk - 1].astype(f32)
+            sender = lax.rem(position + count - kk, count)
+            before += jnp.where(earlier(which, sender, position), value, 0.0)
+            everything += value
+        return before, everything
+
+    def earlier(which, p, mine):
+        return p > mine if which else p < mine
+
+    def step_z(which, i, r, n, peer, source, target):
+        return z_copy(peer, source, target, zs_s.at[which, i, r, n], zs_r.at[which, i, r, n])
+
+    def chain_xyz(which, i, r, now):
+        send, arrived = scan_send.at[which, i, r], zr.at[which, i, r]
+        own = slice(r * part, (r + 1) * part)
+        value = loc[i, own]
+        send[0] = value.astype(bf16)
+        copies = exchange_part("seq_1", nx, which, i, r, 0, 0)
+        yield now + 3.3
+        before, row = collect("seq_1", nx, which, i, r, 0, copies, value)
+        send[1] = row.astype(bf16)
+        copies = exchange_part("seq_0", ny, which, i, r, 1, 1)
+        yield now + 6.4
+        more, _ = collect("seq_0", ny, which, i, r, 1, copies, row)
+        before += more
+        send[2] = before.astype(bf16)
+        send[3] = (before + loc[i, own]).astype(bf16)
+
+        def message(peer):
+            return send.at[2 + jnp.where(earlier(which, zh, peer), 1, 0)]
+
+        az = [
+            step_z(which, i, r, n, peer, message(peer), arrived.at[n])
+            for n, peer in ((0, opposite), (1, up), (2, down))
+        ]
+        yield now + 14.4
+        arrive(az)
+        inc[i, own] = before + arrived[0].astype(f32) + arrived[1].astype(f32) + arrived[2].astype(f32)
+        done(which, now + 14.4)
+
+    def chain_zxy(which, i, r, now):
+        send, arrived = scan_send.at[which, i, r], zr.at[which, i, r]
+        own = slice(r * part, (r + 1) * part)
+        send[0] = loc[i, own].astype(bf16)
         bz = [
-            step_z(up, send.at[3, 0], from_z.at[0], 0),
-            step_z(down, send.at[3, 0], from_z.at[1], 1),
-            step_z(opposite, send.at[3, 0], from_z.at[2], 2),
+            step_z(which, i, r, 0, up, send.at[0], arrived.at[0]),
+            step_z(which, i, r, 1, down, send.at[0], arrived.at[1]),
+            step_z(which, i, r, 2, opposite, send.at[0], arrived.at[2]),
         ]
-        works[0]()
-        before_a, row = collect("seq_1", nx, 0, 0, ax, loc[0])
-        ay = go("seq_0", ny, 0, 1, plain(1, row))
-        works[1]()
-        more, _ = collect("seq_0", ny, 0, 1, ay, row)
-        before_a += more
-        send[2, 0] = before_a.astype(bf16)
-        send[2, 1] = (before_a + loc[0]).astype(bf16)
-
-        def message(peer):
-            return send.at[2, jnp.where(earlier(zh, peer), 1, 0)]
-
-        to_z = zr.at[which, 1]
-        az = [
-            step_z(up, message(opposite).at[top], to_z.at[2, top], 4),
-            step_z(down, message(opposite).at[bottom], to_z.at[2, bottom], 5),
-            step_z(up, message(up).at[bottom], to_z.at[0, bottom], 6),
-            step_z(down, message(down).at[top], to_z.at[1, top], 7),
-        ]
-        before_b, line = jnp.zeros((DK, DK), f32), loc[1]
-        arrive(bz)
+        yield now + 8.0
+        before, line = jnp.zeros((part, DK), f32), loc[i, own]
         for n, sender in ((0, down), (1, up), (2, opposite)):
-            value = from_z[n].astype(f32)
-            before_b += jnp.where(earlier(sender, zh), value, 0.0)
+            bz[n].wait_recv()
+            value = arrived[n].astype(f32)
+            before += jnp.where(earlier(which, sender, zh), value, 0.0)
             line += value
-        bx = go("seq_1", nx, 1, 1, plain(4, line))
-        half_rows = DK // 2
-        az[0].wait_recv()
-        send[5, 1, :half_rows] = (to_z[2, :half_rows].astype(f32) + message(up)[:half_rows].astype(f32)).astype(bf16)
-        az += [step_z(up, send.at[5, 1, top], to_z.at[0, top], 8)]
-        az[1].wait_recv()
-        send[5, 1, half_rows:] = (to_z[2, half_rows:].astype(f32) + message(down)[half_rows:].astype(f32)).astype(bf16)
-        az += [step_z(down, send.at[5, 1, bottom], to_z.at[1, bottom], 9)]
-        more, plane = collect("seq_1", nx, 1, 1, bx, line)
-        before_b += more
-        by = go("seq_0", ny, 1, 2, plain(5, plane))
-        more, _ = collect("seq_0", ny, 1, 2, by, plane)
-        inc[1] = before_b + more
-        arrive(az[2:])
-        inc[0] = before_a + to_z[0].astype(f32) + to_z[1].astype(f32)
+        send[1] = line.astype(bf16)
+        copies = exchange_part("seq_1", nx, which, i, r, 0, 1)
+        yield now + 11.3
+        more, plane = collect("seq_1", nx, which, i, r, 0, copies, line)
+        before += more
+        send[2] = plane.astype(bf16)
+        copies = exchange_part("seq_0", ny, which, i, r, 1, 2)
+        yield now + 14.6
+        more, _ = collect("seq_0", ny, which, i, r, 1, copies, plane)
+        inc[i, own] = before + more
+        done(which, now + 14.6)
+
+    def begin_scan(which, i, now):
+        for r in range(2):
+            chain = chain_zxy if i % 2 else chain_xyz
+            tasks.append((now + 0.01 * r, next(serial), chain(which, i, r, now + 0.5 * r)))
+
+    def work(body, i, first, last):
+        for b in range(first, last):
+            body(b, i, slice(b * BLOCK, (b + 1) * BLOCK), slice(i * DK, (i + 1) * DK))
+        return
+        yield
+
+    def later(now, body, i):
+        for t in range(2):
+            tasks.append((now + 0.7 * t, next(serial), work(body, i, blocks // 2 * t, blocks // 2 * (t + 1))))
+
+    def done(which, now):
+        finished[which] = finished.get(which, 0) + 1
+        if finished[which] < 2 * heads:
+            return
+        if which:
+            for i in range(heads):
+                follow(i)
+            return
+        forward()
+        for i in reversed(range(heads)):
+            begin_scan(1, i, now + 2.0)
+        for i in range(heads):
+            later(now + 2.1, backward_body, i)
 
     def within_body(b, i, at, cols):
         within[b, i] = dot(sc[b, i], v[at, cols], NN)
 
-    halfway_block = blocks // 2
-    scan(
-        0, False,
-        (lambda: unrolled(within_body, 0, halfway_block), lambda: unrolled(within_body, halfway_block, blocks)),
-    )
-
-    for i in range(heads):
-        loc[i] = jnp.zeros((DK, DK), f32)
-
-    def forward_body(b, i, at, cols):
-        prior16 = inc[i].astype(bf16)
-        prior[b, i] = prior16
-        inc[i] += st[b, i]
-        mixed = within[b, i] + dot(q_ref[at, cols], prior16, NN)
-        inverse = 1.0 / jnp.sqrt(jnp.mean(mixed * mixed, axis=-1, keepdims=True) + norm_eps)
-        normed = mixed * inverse
-        attn_ref[at, cols] = normed.astype(bf16)
-        upstream = go_ref[at, cols].astype(f32)
-        inner = jnp.mean(upstream * normed, axis=-1, keepdims=True)
-        grad_mixed = ((upstream - normed * inner) * inverse).astype(bf16)
-        gm[at, cols] = grad_mixed
-        s = dot(q_ref[at, cols], grad_mixed, TN)
-        gs[b, i] = s
-        loc[i] += s
-
-    each_block(forward_body)
-    written[0].start()
+    def forward():
+        places = [
+            (b, i, slice(b * BLOCK, (b + 1) * BLOCK), slice(i * DK, (i + 1) * DK))
+            for b in range(blocks)
+            for i in range(heads)
+        ]
+        for i in range(heads):
+            carried = inc[i]
+            for b in range(blocks):
+                prior[b, i] = carried.astype(bf16)
+                carried = carried + st[b, i]
+        for b, i, at, cols in places:
+            within[b, i] += dot(q_ref[at, cols], prior[b, i], NN)
+        for b, i, at, cols in places:
+            mixed, upstream = within[b, i], go_ref[at, cols].astype(f32)
+            inverse = 1.0 / jnp.sqrt(jnp.mean(mixed * mixed, axis=-1, keepdims=True) + norm_eps)
+            inner = jnp.mean(upstream * mixed, axis=-1, keepdims=True) * inverse
+            normed = mixed * inverse
+            attn_ref[at, cols] = normed.astype(bf16)
+            gm[at, cols] = ((upstream - normed * inner) * inverse).astype(bf16)
+        for b, i, at, cols in places:
+            gs[b, i] = dot(q_ref[at, cols], gm[at, cols], TN)
+        for i in range(heads):
+            total = gs[0, i]
+            for b in range(1, blocks):
+                total = total + gs[b, i]
+            loc[i] = total
 
     def backward_body(b, i, at, cols):
         grad_mixed = gm[at, cols]
@@ -420,22 +488,26 @@
         gkp[b, i] = dot(grad_scores, q_ref[at, cols], TN)
         gvp[b, i] = dot(sc[b, i], grad_mixed, TN)
 
-    scan(
-        1, True,
-        (lambda: unrolled(backward_body, 0, halfway_block), lambda: unrolled(backward_body, halfway_block, blocks)),
-    )
-
-    written[1].start()
-    carried = [inc[i] for i in range(heads)]
-    for b in reversed(range(blocks)):
-        at = slice(b * BLOCK, (b + 1) * BLOCK)
-        for i in range(heads):
-            cols = slice(i * DK, (i + 1) * DK)
-            following16 = carried[i].astype(bf16)
+    def follow(i):
+        carried = inc[i]
+        cols = slice(i * DK, (i + 1) * DK)
+        for b in reversed(range(blocks)):
+            at = slice(b * BLOCK, (b + 1) * BLOCK)
+            following16 = carried.astype(bf16)
             following[b, i] = following16
-            carried[i] = carried[i] + gs[b, i]
+            carried = carried + gs[b, i]
             grad_value = gvp[b, i] + dot(k_ref[at, cols], following16, NN)
             gvt[cols, at] = grad_value.T.astype(bf16)
+
+    for i in range(heads):
+        begin_scan(0, i, 0.0)
+        later(0.1, within_body, i)
+    while tasks:
+        earliest = min(tasks)
+        tasks.remove(earliest)
+        expected = next(earliest[2], None)
+        if expected is not None:
+            tasks.append((expected, earliest[1], earliest[2]))
 
     piece = nz * rows
     side = columns // 2
@@ -501,7 +573,6 @@
         gk_ref[at, cols] = grad_key.astype(bf16)
 
     each_block(key_body)
-    written[2].start()
 
     def summed_a(dx):
         value = pa[0, dx].astype(f32)
@@ -557,11 +628,8 @@
             result += rz[which, kk].astype(f32)
         gl_ref[:, which * side : (which + 1) * side] = result
 
-    written[3].start()
     for copy in sent:
         copy.wait_send()
-    for copy in written:
-        copy.wait()
 
     @pl.loop(0, nl)
     def _(block):
@@ -579,15 +647,10 @@
 
 
 def deliver(*refs):
-    sems = refs[12]
-    inward = [pltpu.make_async_copy(refs[i], refs[8 + i], sems.at[0, i]) for i in range(4)]
-    outward = [pltpu.make_async_copy(refs[8 + i], refs[4 + i], sems.at[1, i]) for i in range(4)]
-    for copy in inward:
+    copies = [pltpu.make_async_copy(refs[i], refs[4 + i], refs[8].at[i]) for i in range(4)]
+    for copy in copies:
         copy.start()
-    for copy, following in zip(inward, outward):
-        copy.wait()
-        following.start()
-    for copy in outward:
+    for copy in copies:
         copy.wait()
 
 
@@ -602,8 +665,6 @@
     dma = pltpu.SemaphoreType.DMA
     most = max(ny, nx, nz) - 1
     scratch = [
-        *[pltpu.VMEM((tokens, columns), bf16)] * 3,
-        pltpu.VMEM(latent.shape, f32),
         pltpu.VMEM(latent.shape, f32),
         pltpu.VMEM((tokens, columns), bf16),
         pltpu.VMEM((tokens, columns), bf16),
@@ -625,9 +686,9 @@
         pltpu.VMEM((blocks, heads, BLOCK, DK), f32),
         pltpu.VMEM((columns, tokens), bf16),
         pltpu.VMEM((heads, DK, DK), f32),
-        pltpu.VMEM((2, 6, 2, DK, DK), bf16),
-        pltpu.VMEM((2, 6, most, DK, DK), bf16),
-        pltpu.VMEM((2, 2, 3, DK, DK), bf16),
+        pltpu.VMEM((2, heads, 2, 4, DK // 2, DK), bf16),
+        pltpu.VMEM((2, heads, 2, 2, most, DK // 2, DK), bf16),
+        pltpu.VMEM((2, heads, 2, 3, DK // 2, DK), bf16),
         pltpu.VMEM((heads, DK, DK), f32),
         pltpu.VMEM((ny, nx, side, piece), bf16),
         pltpu.VMEM((ny, nx, side, piece), bf16),
@@ -641,14 +702,13 @@
         pltpu.VMEM((2, piece, side), f32),
         pltpu.VMEM((2, nz - 1, rows, side), bf16),
         dma((5,)),
-        dma((4,)),
-        dma((2, most)), dma((2, most)),
+        dma((6,)), dma((6,)),
         dma((2, most)), dma((2, most)),
         dma((2, most)), dma((2, most)),
         dma((nl, CHUNKS)), dma((nl, CHUNKS)), dma((nl, CHUNKS)),
         dma((nl, CHUNKS)), dma((nl, CHUNKS)),
-        dma((2, 6, most)), dma((2, 6, most)),
-        dma((2, 10)), dma((2, 10)),
+        dma((2, heads, 2, 2, most)), dma((2, heads, 2, 2, most)),
+        dma((2, heads, 2, 3)), dma((2, heads, 2, 3)),
         dma((2, 4, 6)), dma((2, 4, 6)),
         dma((4, most)), dma((4, most)),
     ]
@@ -657,23 +717,19 @@
         functools.partial(kernel, sizes),
         out_shape=(like, like, like, jax.ShapeDtypeStruct(latent.shape, f32)),
         in_specs=[pl.BlockSpec(memory_space=pltpu.HBM)] * 5,
-        out_specs=(pl.BlockSpec(memory_space=pltpu.HBM),) * 4,
+        out_specs=(pl.BlockSpec(memory_space=pltpu.VMEM),) * 4,
         scratch_shapes=scratch,
         compiler_params=pltpu.CompilerParams(
-            collective_id=0, has_side_effects=True, vmem_limit_bytes=60 << 20
+            collective_id=0, has_side_effects=True, vmem_limit_bytes=40 << 20
         ),
-    )(inputs, latent, queries, keys, grad_out)
+    )(*(pltpu.with_memory_space_constraint(a, pltpu.HBM) for a in (inputs, latent, queries, keys, grad_out)))
     return pl.pallas_call(
         deliver,
         out_shape=(like, like, like, jax.ShapeDtypeStruct(latent.shape, f32)),
-        in_specs=[pl.BlockSpec(memory_space=pltpu.HBM)] * 4,
+        in_specs=[pl.BlockSpec(memory_space=pltpu.VMEM)] * 4,
         out_specs=(pl.BlockSpec(memory_space=pltpu.HBM),) * 4,
-        scratch_shapes=[
-            *[pltpu.VMEM(queries.shape, bf16)] * 3,
-            pltpu.VMEM(latent.shape, f32),
-            pltpu.SemaphoreType.DMA((2, 4)),
-        ],
-        compiler_params=pltpu.CompilerParams(vmem_limit_bytes=60 << 20),
+        scratch_shapes=[pltpu.SemaphoreType.DMA((4,))],
+        compiler_params=pltpu.CompilerParams(vmem_limit_bytes=4 << 20),
     )(*results)
 
 

time: 126 us -> 122 us (0.968)
  Pallas kernels: 124 us -> 121 us
    pallas_call x1, Pallas kernels: 122 us -> 120 us  [per_device(): pl.pallas_call(functools.partial(kernel, sizes), out_shape=(like, like, l...]
where the time goes in v3:
time: 122 us; the launch traced here: 121 us
  Pallas kernels  121 us (99%)
    pallas_call x1, Pallas kernels, per_device(): pl.pallas_call(functools.partial(kernel, sizes), out_shape=(like, like, l...  120 us

profile of v3, /device:TPU:6, one launch (start us, length us, event | category | flops | bytes accessed | tf_op | source)
XLA Modules:
  0.0 121.4 jit_solution(10948844766015964186)
XLA Ops:
  0.6 119.8 %shard_map.84 = (bf16[512,256]{1,0:T(8,128)(2,1)S(1)}, bf16[512,256]{1,0:T(8,128)(2,1)S(1)}, bf16[512,256]{1,0:T(8,128)(2,1)S(1)}, f32[64,256]{1,0:T(8,128)S(1)}) custom-call(bf16[512,512]{1,0:T(8,128)(2,1)} %x_in.1, f32[64,256]{1,0:T(8,128)} %latent_in.1, bf16[512,256]{1,0:T(8,128)(2,1)} %q_in.1, bf16[512,256]{1,0:T(8,128)(2,1)} %k_in.1, bf16[512,256]{1,0:T(8,128)(2,1)} %go_in.1), custom_call_target="tpu_custom_call" | custom-call | tf_op jit(solution)/shard_map/pallas_call | solution.py:716
  120.5 0.9 shard_map.85

commit v4 on v3

--- a/solution.py
+++ b/solution.py
@@ -14,8 +14,8 @@
 HEAD = ("head_0", "head_1")
 SEQ = ("seq_0", "seq_1", "seq_2")
 ID = pl.DeviceIdType.MESH
-CHUNKS = 8
-EARLY = 3
+CHUNKS = 4
+EARLY = 2
 
 absmean_eps = 1e-05
 norm_eps = 1e-06
@@ -31,22 +31,22 @@
 NN, NT, TN = (1, 0), (1, 1), (0, 0)
 
 
-def exchange(axis, count, source, target, send, recv):
+def exchange(axis, count, source, target, send, recv, shared=False):
     position = lax.axis_index(axis)
-    copies = []
-    for kk in range(1, count):
+    copies = {}
+    for kk in sorted(range(1, count), key=lambda kk: abs(2 * kk - count)):
         peer = lax.rem(position + kk, count)
         copy = pltpu.make_async_remote_copy(
             src_ref=source(peer),
             dst_ref=target(kk),
-            send_sem=send.at[kk - 1],
+            send_sem=send if shared else send.at[kk - 1],
             recv_sem=recv.at[kk - 1],
             device_id={axis: peer},
             device_id_type=ID,
         )
         copy.start()
-        copies.append(copy)
-    return copies
+        copies[kk] = copy
+    return [copies[kk] for kk in range(1, count)]
 
 
 def arrive(copies):
@@ -69,7 +69,7 @@
     heads = columns // DK
     blocks = tokens // BLOCK
     step = tokens // CHUNKS
-    sent = []
+    sent, left = [], []
 
     fetches = [
         pltpu.make_async_copy(latent_in, latent_ref, own_sem.at[0]),
@@ -110,13 +110,14 @@
     up, down = lax.rem(zh + 1, nz), lax.rem(zh + nz - 1, nz)
     opposite = lax.rem(zh + 2, nz)
 
-    def z_copy(peer, source, target, send, recv):
+    def z_copy(peer, source, target, send, recv, alone=True):
         copy = pltpu.make_async_remote_copy(
             src_ref=source, dst_ref=target, send_sem=send, recv_sem=recv,
             device_id={"seq_2": peer}, device_id_type=ID,
         )
         copy.start()
-        sent.append(copy)
+        if alone:
+            sent.append(copy)
         return copy
 
     def w_copy(peer, ref, at, n):
@@ -137,7 +138,7 @@
         return pltpu.make_async_remote_copy(
             src_ref=place,
             dst_ref=place,
-            send_sem=(xp_s if up else xm_s).at[block, j],
+            send_sem=(xp_s if up else xm_s).at[block],
             recv_sem=xl_r.at[block, j],
             device_id={"head_0": zl + 1 if up else zl - 1},
             device_id_type=ID,
@@ -148,7 +149,7 @@
         return pltpu.make_async_remote_copy(
             src_ref=place,
             dst_ref=place,
-            send_sem=xs_s.at[block, j],
+            send_sem=xs_s.at[block],
             recv_sem=xs_r.at[block, j],
             device_id={"head_1": 1 - cc},
             device_id_type=ID,
@@ -255,7 +256,7 @@
                 line_copy(far, j, True).wait_recv()
                 side_copy(far, j).start()
 
-    share_far(0, 2)
+    share_far(0, 1)
 
     def magnitude(s, total):
         both = jnp.abs(wa[s].astype(f32)) + jnp.abs(wb[s].astype(f32))
@@ -277,7 +278,7 @@
             wt[pl.ds(at, half)] = ternary(wa[p * nz + z])
             wt[pl.ds(pl.multiple_of(at + half, half), half)] = ternary(wb[other * nz + z])
 
-    share_far(2, 3)
+    share_far(1, 2)
     acc[...] = jnp.zeros_like(acc)
 
     def features(block, core):
@@ -295,7 +296,7 @@
             def _(core):
                 acc[...] += dot(xg[block, core], features(block, core), NN)
 
-    share_far(3, CHUNKS // 2 + 1)
+    share_far(2, CHUNKS // 2 + 1)
 
     @at_end
     def _():
@@ -322,6 +323,20 @@
         side_copy(far, CHUNKS - 1).wait_recv()
         multiply(1 - cc, CHUNKS - 1)
 
+    def all_left(ref, semaphore):
+        pltpu.make_async_remote_copy(
+            src_ref=ref, dst_ref=ref, send_sem=semaphore, recv_sem=semaphore,
+            device_id={"head_1": 1 - cc}, device_id_type=ID,
+        ).wait_send()
+
+    @pl.when(zl == nl - 2)
+    def _():
+        all_left(xg.at[0, cc], xp_s.at[0])
+
+    @pl.when(zl == 1)
+    def _():
+        all_left(xg.at[nl - 1, cc], xm_s.at[nl - 1])
+
     v[...] = acc[...].astype(bf16)
 
     totals = [jnp.zeros((DK, DK), f32)] * heads
@@ -342,9 +357,9 @@
     def exchange_part(axis, count, which, i, r, stage, slot):
         copies = exchange(
             axis, count, lambda p: scan_send.at[which, i, r, slot], lambda kk: scan_recv.at[which, i, r, stage, kk - 1],
-            scan_s.at[which, i, r, stage], scan_r.at[which, i, r, stage],
+            scan_s.at[which, i, r, stage], scan_r.at[which, i, r, stage], True,
         )
-        sent.extend(copies)
+        left.append((scan_send.at[which, i, r, 0 : count - 1], scan_s.at[which, i, r, stage]))
         return copies
 
     def collect(axis, count, which, i, r, stage, copies, mine):
@@ -362,7 +377,9 @@
         return p > mine if which else p < mine
 
     def step_z(which, i, r, n, peer, source, target):
-        return z_copy(peer, source, target, zs_s.at[which, i, r, n], zs_r.at[which, i, r, n])
+        if n == 0:
+            left.append((scan_send.at[which, i, r, 0 : nz - 1], zs_s.at[which, i, r]))
+        return z_copy(peer, source, target, zs_s.at[which, i, r], zs_r.at[which, i, r, n], False)
 
     def chain_xyz(which, i, r, now):
         send, arrived = scan_send.at[which, i, r], zr.at[which, i, r]
@@ -397,13 +414,12 @@
         own = slice(r * part, (r + 1) * part)
         send[0] = loc[i, own].astype(bf16)
         bz = [
-            step_z(which, i, r, 0, up, send.at[0], arrived.at[0]),
-            step_z(which, i, r, 1, down, send.at[0], arrived.at[1]),
-            step_z(which, i, r, 2, opposite, send.at[0], arrived.at[2]),
+            step_z(which, i, r, n, peer, send.at[0], arrived.at[n])
+            for n, peer in ((0, opposite), (1, up), (2, down))
         ]
         yield now + 8.0
         before, line = jnp.zeros((part, DK), f32), loc[i, own]
-        for n, sender in ((0, down), (1, up), (2, opposite)):
+        for n, sender in ((0, opposite), (1, down), (2, up)):
             bz[n].wait_recv()
             value = arrived[n].astype(f32)
             before += jnp.where(earlier(which, sender, zh), value, 0.0)
@@ -525,11 +541,10 @@
         peer = lax.rem(position + (1 if forward else count - 1), count)
         copy = pltpu.make_async_remote_copy(
             src_ref=source, dst_ref=target,
-            send_sem=g1_s.at[which, k, n], recv_sem=g1_r.at[which, k, n],
+            send_sem=g1_s.at[which, k], recv_sem=g1_r.at[which, k, n],
             device_id={axis: peer}, device_id_type=ID,
         )
         copy.start()
-        sent.append(copy)
         ring[which, k, n] = copy
 
     def begin(which, distance, k, source, target):
@@ -565,14 +580,7 @@
         begin(1, dx, dy, pb.at[dy, dx], rb1)
         if n == 11:
             pass_both(2)
-    for k in (1, 3, 0):
-        pass_both(k)
-
-    def key_body(b, i, at, cols):
-        grad_key = gkp[b, i] + dot(v[at, cols], following[b, i], NT)
-        gk_ref[at, cols] = grad_key.astype(bf16)
-
-    each_block(key_body)
+    left += [(ref.at[0:3, 0], g1_s.at[which, k]) for which, ref in ((0, pa), (1, pb)) for k in range(4)]
 
     def summed_a(dx):
         value = pa[0, dx].astype(f32)
@@ -597,13 +605,26 @@
         return copy
 
     a2, b2 = [], []
-    for k in (2, 1, 3):
-        if k < nx:
-            sa2[k - 1] = summed_a(k).astype(bf16)
-            a2.append(second("seq_1", xx, nx, k, sa2, ra2, 0))
-        if k < ny:
-            sb2[k - 1] = summed_b(k).astype(bf16)
-            b2.append(second("seq_0", yy, ny, k, sb2, rb2, 1))
+
+    def second_both(k):
+        sa2[k - 1] = summed_a(k).astype(bf16)
+        a2.append(second("seq_1", xx, nx, k, sa2, ra2, 0))
+        sb2[k - 1] = summed_b(k).astype(bf16)
+        b2.append(second("seq_0", yy, ny, k, sb2, rb2, 1))
+
+    pass_both(1)
+    second_both(2)
+    pass_both(3)
+    second_both(1)
+    pass_both(0)
+    second_both(3)
+
+    def key_body(b, i, at, cols):
+        grad_key = gkp[b, i] + dot(v[at, cols], following[b, i], NT)
+        gk_ref[at, cols] = grad_key.astype(bf16)
+
+    each_block(key_body)
+
     final_a, final_b = summed_a(0), summed_b(0)
 
     def last(final, second_copies, received, which):
@@ -631,19 +652,23 @@
     for copy in sent:
         copy.wait_send()
 
+    for ref, semaphore in left:
+        all_left(ref, semaphore)
+
     @pl.loop(0, nl)
     def _(block):
-        @pl.loop(0, CHUNKS)
-        def _(j):
-            side_copy(block, j).wait_send()
-
-            @pl.when(jnp.logical_and(block <= zl, zl < nl - 1))
-            def _():
-                line_copy(block, j, True).wait_send()
-
-            @pl.when(jnp.logical_and(block >= zl, zl > 0))
-            def _():
-                line_copy(block, j, False).wait_send()
+        place = xg.at[block, cc]
+        all_left(place, xs_s.at[block])
+        ahead = jnp.logical_and(zl == nl - 2, block == 0)
+        behind = jnp.logical_and(zl == 1, block == nl - 1)
+
+        @pl.when(jnp.logical_and(jnp.logical_and(block <= zl, zl < nl - 1), jnp.logical_not(ahead)))
+        def _():
+            all_left(place, xp_s.at[block])
+
+        @pl.when(jnp.logical_and(jnp.logical_and(block >= zl, zl > 0), jnp.logical_not(behind)))
+        def _():
+            all_left(place, xm_s.at[block])
 
 
 def deliver(*refs):
@@ -705,11 +730,11 @@
         dma((6,)), dma((6,)),
         dma((2, most)), dma((2, most)),
         dma((2, most)), dma((2, most)),
-        dma((nl, CHUNKS)), dma((nl, CHUNKS)), dma((nl, CHUNKS)),
+        dma((nl,)), dma((nl,)), dma((nl,)),
         dma((nl, CHUNKS)), dma((nl, CHUNKS)),
-        dma((2, heads, 2, 2, most)), dma((2, heads, 2, 2, most)),
-        dma((2, heads, 2, 3)), dma((2, heads, 2, 3)),
-        dma((2, 4, 6)), dma((2, 4, 6)),
+        dma((2, heads, 2, 2)), dma((2, heads, 2, 2, most)),
+        dma((2, heads, 2)), dma((2, heads, 2, 3)),
+        dma((2, 4)), dma((2, 4, 6)),
         dma((4, most)), dma((4, most)),
     ]
     like = jax.ShapeDtypeStruct(queries.shape, bf16)

time: 122 us -> 118 us (0.967)
  Pallas kernels: 121 us -> 117 us
    pallas_call x1, Pallas kernels: 120 us -> 116 us  [per_device(): pl.pallas_call(functools.partial(kernel, sizes), out_shape=(like, like, l...]
where the time goes in v4:
time: 118 us
  Pallas kernels  117 us (99%)
    pallas_call x1, Pallas kernels, per_device(): pl.pallas_call(functools.partial(kernel, sizes), out_shape=(like, like, l...  116 us

profile of v4, /device:TPU:6, one launch (start us, length us, event | category | flops | bytes accessed | tf_op | source)
XLA Modules:
  0.0 117.6 jit_solution(17974530948049923608)
XLA Ops:
  0.6 116.1 %shard_map.84 = (bf16[512,256]{1,0:T(8,128)(2,1)S(1)}, bf16[512,256]{1,0:T(8,128)(2,1)S(1)}, bf16[512,256]{1,0:T(8,128)(2,1)S(1)}, f32[64,256]{1,0:T(8,128)S(1)}) custom-call(bf16[512,512]{1,0:T(8,128)(2,1)} %x_in.1, f32[64,256]{1,0:T(8,128)} %latent_in.1, bf16[512,256]{1,0:T(8,128)(2,1)} %q_in.1, bf16[512,256]{1,0:T(8,128)(2,1)} %k_in.1, bf16[512,256]{1,0:T(8,128)(2,1)} %go_in.1), custom_call_target="tpu_custom_call" | custom-call | tf_op jit(solution)/shard_map/pallas_call | solution.py:741
  116.7 0.9 shard_map.85

commit v5 on v4

--- a/solution.py
+++ b/solution.py
@@ -16,6 +16,7 @@
 ID = pl.DeviceIdType.MESH
 CHUNKS = 4
 EARLY = 2
+PIECES = 1
 
 absmean_eps = 1e-05
 norm_eps = 1e-06
@@ -40,7 +41,7 @@
             src_ref=source(peer),
             dst_ref=target(kk),
             send_sem=send if shared else send.at[kk - 1],
-            recv_sem=recv.at[kk - 1],
+            recv_sem=recv if shared else recv.at[kk - 1],
             device_id={axis: peer},
             device_id_type=ID,
         )
@@ -329,6 +330,12 @@
             device_id={"head_1": 1 - cc}, device_id_type=ID,
         ).wait_send()
 
+    def all_arrived(ref, semaphore):
+        pltpu.make_async_remote_copy(
+            src_ref=ref, dst_ref=ref, send_sem=semaphore, recv_sem=semaphore,
+            device_id={"head_1": 1 - cc}, device_id_type=ID,
+        ).wait_recv()
+
     @pl.when(zl == nl - 2)
     def _():
         all_left(xg.at[0, cc], xp_s.at[0])
@@ -350,7 +357,7 @@
     for i in range(heads):
         loc[i] = totals[i]
 
-    part = DK // 2
+    part = DK // PIECES
     tasks, serial = [], itertools.count()
     finished = {}
 
@@ -365,8 +372,8 @@
     def collect(axis, count, which, i, r, stage, copies, mine):
         position = lax.axis_index(axis)
         before, everything = jnp.zeros((part, DK), f32), mine
+        all_arrived(scan_recv.at[which, i, r, stage, 0 : count - 1], scan_r.at[which, i, r, stage])
         for kk in range(1, count):
-            copies[kk - 1].wait_recv()
             value = scan_recv[which, i, r, stage, kk - 1].astype(f32)
             sender = lax.rem(position + count - kk, count)
             before += jnp.where(earlier(which, sender, position), value, 0.0)
@@ -379,7 +386,7 @@
     def step_z(which, i, r, n, peer, source, target):
         if n == 0:
             left.append((scan_send.at[which, i, r, 0 : nz - 1], zs_s.at[which, i, r]))
-        return z_copy(peer, source, target, zs_s.at[which, i, r], zs_r.at[which, i, r, n], False)
+        return z_copy(peer, source, target, zs_s.at[which, i, r], zs_r.at[which, i, r], False)
 
     def chain_xyz(which, i, r, now):
         send, arrived = scan_send.at[which, i, r], zr.at[which, i, r]
@@ -400,12 +407,10 @@
         def message(peer):
             return send.at[2 + jnp.where(earlier(which, zh, peer), 1, 0)]
 
-        az = [
+        for n, peer in ((0, opposite), (1, up), (2, down)):
             step_z(which, i, r, n, peer, message(peer), arrived.at[n])
-            for n, peer in ((0, opposite), (1, up), (2, down))
-        ]
         yield now + 14.4
-        arrive(az)
+        all_arrived(arrived, zs_r.at[which, i, r])
         inc[i, own] = before + arrived[0].astype(f32) + arrived[1].astype(f32) + arrived[2].astype(f32)
         done(which, now + 14.4)
 
@@ -413,14 +418,12 @@
         send, arrived = scan_send.at[which, i, r], zr.at[which, i, r]
         own = slice(r * part, (r + 1) * part)
         send[0] = loc[i, own].astype(bf16)
-        bz = [
+        for n, peer in ((0, opposite), (1, up), (2, down)):
             step_z(which, i, r, n, peer, send.at[0], arrived.at[n])
-            for n, peer in ((0, opposite), (1, up), (2, down))
-        ]
         yield now + 8.0
         before, line = jnp.zeros((part, DK), f32), loc[i, own]
+        all_arrived(arrived, zs_r.at[which, i, r])
         for n, sender in ((0, opposite), (1, down), (2, up)):
-            bz[n].wait_recv()
             value = arrived[n].astype(f32)
             before += jnp.where(earlier(which, sender, zh), value, 0.0)
             line += value
@@ -437,7 +440,7 @@
         done(which, now + 14.6)
 
     def begin_scan(which, i, now):
-        for r in range(2):
+        for r in range(PIECES):
             chain = chain_zxy if i % 2 else chain_xyz
             tasks.append((now + 0.01 * r, next(serial), chain(which, i, r, now + 0.5 * r)))
 
@@ -453,7 +456,7 @@
 
     def done(which, now):
         finished[which] = finished.get(which, 0) + 1
-        if finished[which] < 2 * heads:
+        if finished[which] < PIECES * heads:
             return
         if which:
             for i in range(heads):
@@ -541,7 +544,7 @@
         peer = lax.rem(position + (1 if forward else count - 1), count)
         copy = pltpu.make_async_remote_copy(
             src_ref=source, dst_ref=target,
-            send_sem=g1_s.at[which, k], recv_sem=g1_r.at[which, k, n],
+            send_sem=g1_s.at[which, k], recv_sem=g1_r.at[which, k, min(n, 2)],
             device_id={axis: peer}, device_id_type=ID,
         )
         copy.start()
@@ -584,33 +587,29 @@
 
     def summed_a(dx):
         value = pa[0, dx].astype(f32)
-        for n in (2, 3, 4, 5):
-            ring[0, dx, n].wait_recv()
+        all_arrived(ra1.at[0:2, dx], g1_r.at[0, dx, 2])
         return value + ra1[0, dx].astype(f32) + ra1[1, dx].astype(f32)
 
     def summed_b(dy):
         value = pb[dy, 0].astype(f32)
-        for n in (2, 3, 4, 5):
-            ring[1, dy, n].wait_recv()
+        all_arrived(rb1.at[0:2, dy], g1_r.at[1, dy, 2])
         return value + rb1[0, dy].astype(f32) + rb1[1, dy].astype(f32)
 
     def second(axis, position, count, k, source, target, which):
         copy = pltpu.make_async_remote_copy(
             src_ref=source.at[k - 1], dst_ref=target.at[k - 1],
-            send_sem=g_s.at[which, k - 1], recv_sem=g_r.at[which, k - 1],
+            send_sem=g_s.at[which], recv_sem=g_r.at[which],
             device_id={axis: lax.rem(position + k, count)}, device_id_type=ID,
         )
         copy.start()
-        sent.append(copy)
-        return copy
-
-    a2, b2 = [], []
+
+    left += [(sa2, g_s.at[0]), (sb2, g_s.at[1])]
 
     def second_both(k):
         sa2[k - 1] = summed_a(k).astype(bf16)
-        a2.append(second("seq_1", xx, nx, k, sa2, ra2, 0))
+        second("seq_1", xx, nx, k, sa2, ra2, 0)
         sb2[k - 1] = summed_b(k).astype(bf16)
-        b2.append(second("seq_0", yy, ny, k, sb2, rb2, 1))
+        second("seq_0", yy, ny, k, sb2, rb2, 1)
 
     pass_both(1)
     second_both(2)
@@ -627,24 +626,24 @@
 
     final_a, final_b = summed_a(0), summed_b(0)
 
-    def last(final, second_copies, received, which):
-        for copy in second_copies:
-            copy.wait_recv()
-        for kk in range(len(second_copies)):
+    def last(final, received, which):
+        all_arrived(received, g_r.at[which])
+        for kk in range(received.shape[0]):
             final += received[kk].astype(f32)
         final = final.T
         tzf[which] = final
         tz[which] = final.astype(bf16)
-        return exchange(
+        left.append((tz.at[which, 0 : (nz - 1) * rows], g_s.at[2 + which]))
+        exchange(
             "seq_2", nz, lambda p: tz.at[which, pl.ds(pl.multiple_of(p * rows, rows), rows)],
-            lambda kk: rz.at[which, kk - 1], g_s.at[2 + which], g_r.at[2 + which],
+            lambda kk: rz.at[which, kk - 1], g_s.at[2 + which], g_r.at[2 + which], True,
         )
 
-    z3 = [last(final_a, a2, ra2, 0), last(final_b, b2, rb2, 1)]
-    for which, copies in enumerate(z3):
-        sent += copies
+    last(final_a, ra2, 0)
+    last(final_b, rb2, 1)
+    for which in range(2):
         result = tzf[which, pl.ds(pl.multiple_of(zh * rows, rows), rows)]
-        arrive(copies)
+        all_arrived(rz.at[which], g_r.at[2 + which])
         for kk in range(nz - 1):
             result += rz[which, kk].astype(f32)
         gl_ref[:, which * side : (which + 1) * side] = result
@@ -711,9 +710,9 @@
         pltpu.VMEM((blocks, heads, BLOCK, DK), f32),
         pltpu.VMEM((columns, tokens), bf16),
         pltpu.VMEM((heads, DK, DK), f32),
-        pltpu.VMEM((2, heads, 2, 4, DK // 2, DK), bf16),
-        pltpu.VMEM((2, heads, 2, 2, most, DK // 2, DK), bf16),
-        pltpu.VMEM((2, heads, 2, 3, DK // 2, DK), bf16),
+        pltpu.VMEM((2, heads, PIECES, 4, DK // PIECES, DK), bf16),
+        pltpu.VMEM((2, heads, PIECES, 2, most, DK // PIECES, DK), bf16),
+        pltpu.VMEM((2, heads, PIECES, 3, DK // PIECES, DK), bf16),
         pltpu.VMEM((heads, DK, DK), f32),
         pltpu.VMEM((ny, nx, side, piece), bf16),
         pltpu.VMEM((ny, nx, side, piece), bf16),
@@ -732,10 +731,10 @@
         dma((2, most)), dma((2, most)),
         dma((nl,)), dma((nl,)), dma((nl,)),
         dma((nl, CHUNKS)), dma((nl, CHUNKS)),
-        dma((2, heads, 2, 2)), dma((2, heads, 2, 2, most)),
-        dma((2, heads, 2)), dma((2, heads, 2, 3)),
-        dma((2, 4)), dma((2, 4, 6)),
-        dma((4, most)), dma((4, most)),
+        dma((2, heads, PIECES, 2)), dma((2, heads, PIECES, 2)),
+        dma((2, heads, PIECES)), dma((2, heads, PIECES)),
+        dma((2, 4)), dma((2, 4, 3)),
+        dma((4,)), dma((4,)),
     ]
     like = jax.ShapeDtypeStruct(queries.shape, bf16)
     results = pl.pallas_call(

time: 118 us -> 117 us (level)
  no operation moved by 1% of the time
where the time goes in v5:
time: 117 us
  Pallas kernels  116 us (99%)
    pallas_call x1, Pallas kernels, per_device(): pl.pallas_call(functools.partial(kernel, sizes), out_shape=(like, like, l...  115 us

profile of v5, /device:TPU:6, one launch (start us, length us, event | category | flops | bytes accessed | tf_op | source)
XLA Modules:
  0.0 116.6 jit_solution(16124936076037117291)
XLA Ops:
  0.6 115.1 %shard_map.84 = (bf16[512,256]{1,0:T(8,128)(2,1)S(1)}, bf16[512,256]{1,0:T(8,128)(2,1)S(1)}, bf16[512,256]{1,0:T(8,128)(2,1)S(1)}, f32[64,256]{1,0:T(8,128)S(1)}) custom-call(bf16[512,512]{1,0:T(8,128)(2,1)} %x_in.1, f32[64,256]{1,0:T(8,128)} %latent_in.1, bf16[512,256]{1,0:T(8,128)(2,1)} %q_in.1, bf16[512,256]{1,0:T(8,128)(2,1)} %k_in.1, bf16[512,256]{1,0:T(8,128)(2,1)} %go_in.1), custom_call_target="tpu_custom_call" | custom-call | tf_op jit(solution)/shard_map/pallas_call | solution.py:740
  115.7 0.9 shard_map.85

commit v6 on v5

--- a/solution.py
+++ b/solution.py
@@ -131,6 +131,18 @@
         w_copy(down, wa, at_a + zh, 3),
     ]
 
+    def all_left(ref, semaphore):
+        pltpu.make_async_remote_copy(
+            src_ref=ref, dst_ref=ref, send_sem=semaphore, recv_sem=semaphore,
+            device_id={"head_1": 1 - cc}, device_id_type=ID,
+        ).wait_send()
+
+    def all_arrived(ref, semaphore):
+        pltpu.make_async_remote_copy(
+            src_ref=ref, dst_ref=ref, send_sem=semaphore, recv_sem=semaphore,
+            device_id={"head_1": 1 - cc}, device_id_type=ID,
+        ).wait_recv()
+
     def rows_of(ref, j):
         return ref.at[pl.ds(pl.multiple_of(j * step, step), step)]
 
@@ -229,21 +241,21 @@
     arrive(wz[2:])
     mine_a = wa.at[pl.ds(at_a, nz)]
     mine_b = wb.at[pl.ds(at_b, nz)]
-    w2a = exchange("seq_1", nx, lambda p: mine_a, lambda kk: mine_a, w2_s.at[0], w2_r.at[0])
-    w2b = exchange("seq_0", ny, lambda p: mine_b, lambda kk: mine_b, w2_s.at[1], w2_r.at[1])
-    sent += w2a + w2b
+    exchange("seq_1", nx, lambda p: mine_a, lambda kk: mine_a, w2_s.at[0], w2_r.at[0], True)
+    exchange("seq_0", ny, lambda p: mine_b, lambda kk: mine_b, w2_s.at[1], w2_r.at[1], True)
+    left += [(wa.at[0 : 3 * nz], w2_s.at[0]), (wb.at[0 : 3 * nz], w2_s.at[1])]
     relay(1, CHUNKS // 2, CHUNKS)
     row_a = wa.at[pl.ds(yy * nx * nz, nx * nz)]
     row_b = wb.at[pl.ds(xx * ny * nz, ny * nz)]
-    arrive(w2a)
-    w3a = exchange("seq_0", ny, lambda p: row_a, lambda kk: row_a, w3_s.at[0], w3_r.at[0])
-    arrive(w2b)
-    w3b = exchange("seq_1", nx, lambda p: row_b, lambda kk: row_b, w3_s.at[1], w3_r.at[1])
-    sent += w3a + w3b
+    all_arrived(wa.at[0 : 3 * nz], w2_r.at[0])
+    exchange("seq_0", ny, lambda p: row_a, lambda kk: row_a, w3_s.at[0], w3_r.at[0], True)
+    all_arrived(wb.at[0 : 3 * nz], w2_r.at[1])
+    exchange("seq_1", nx, lambda p: row_b, lambda kk: row_b, w3_s.at[1], w3_r.at[1], True)
+    left += [(wa.at[0 : 3 * nx * nz], w3_s.at[0]), (wb.at[0 : 3 * ny * nz], w3_s.at[1])]
     for distance in range(2, nl - 1):
         relay(distance, 0, CHUNKS)
-    arrive(w3a)
-    arrive(w3b)
+    all_arrived(wa.at[0 : 3 * nx * nz], w3_r.at[0])
+    all_arrived(wb.at[0 : 3 * ny * nz], w3_r.at[1])
     far = nl - 1 - zl
 
     def at_end(body):
@@ -323,18 +335,6 @@
             multiply(cc, j)
         side_copy(far, CHUNKS - 1).wait_recv()
         multiply(1 - cc, CHUNKS - 1)
-
-    def all_left(ref, semaphore):
-        pltpu.make_async_remote_copy(
-            src_ref=ref, dst_ref=ref, send_sem=semaphore, recv_sem=semaphore,
-            device_id={"head_1": 1 - cc}, device_id_type=ID,
-        ).wait_send()
-
-    def all_arrived(ref, semaphore):
-        pltpu.make_async_remote_copy(
-            src_ref=ref, dst_ref=ref, send_sem=semaphore, recv_sem=semaphore,
-            device_id={"head_1": 1 - cc}, device_id_type=ID,
-        ).wait_recv()
 
     @pl.when(zl == nl - 2)
     def _():
@@ -727,8 +727,8 @@
         pltpu.VMEM((2, nz - 1, rows, side), bf16),
         dma((5,)),
         dma((6,)), dma((6,)),
-        dma((2, most)), dma((2, most)),
-        dma((2, most)), dma((2, most)),
+        dma((2,)), dma((2,)),
+        dma((2,)), dma((2,)),
         dma((nl,)), dma((nl,)), dma((nl,)),
         dma((nl, CHUNKS)), dma((nl, CHUNKS)),
         dma((2, heads, PIECES, 2)), dma((2, heads, PIECES, 2)),

time: 117 us -> 117 us (level)
  no operation moved by 1% of the time
where the time goes in v6:
time: 117 us; the launch traced here: 116 us
  Pallas kernels  116 us (99%)
    pallas_call x1, Pallas kernels, per_device(): pl.pallas_call(functools.partial(kernel, sizes), out_shape=(like, like, l...  115 us

profile of v6, /device:TPU:6, one launch (start us, length us, event | category | flops | bytes accessed | tf_op | source)
XLA Modules:
  0.0 116.5 jit_solution(9050583830169245069)
XLA Ops:
  0.6 114.9 %shard_map.84 = (bf16[512,256]{1,0:T(8,128)(2,1)S(1)}, bf16[512,256]{1,0:T(8,128)(2,1)S(1)}, bf16[512,256]{1,0:T(8,128)(2,1)S(1)}, f32[64,256]{1,0:T(8,128)S(1)}) custom-call(bf16[512,512]{1,0:T(8,128)(2,1)} %x_in.1, f32[64,256]{1,0:T(8,128)} %latent_in.1, bf16[512,256]{1,0:T(8,128)(2,1)} %q_in.1, bf16[512,256]{1,0:T(8,128)(2,1)} %k_in.1, bf16[512,256]{1,0:T(8,128)(2,1)} %go_in.1), custom_call_target="tpu_custom_call" | custom-call | tf_op jit(solution)/shard_map/pallas_call | solution.py:740
  115.6 0.9 shard_map.85
